TPU v7x, 128 devices: a whole 4x4x4 slice. The times are simulated.
128 devices in a mesh: seq: 16 (over z, x), head: 8 (over y, core).
Axes of the slice: x: 4, y: 4, z: 4, core: 2. Of those that a mesh axis runs over, the one named last changes fastest.
Arguments:
- tokens: bfloat16 [16384, 4096], P('seq'), may hold values from -6 to 6
- w_query: bfloat16 [4096, 4096], P(None, 'head'), may hold values from -0.09375 to 0.09375
- w_key: bfloat16 [4096, 4096], P(None, 'head'), may hold values from -0.09375 to 0.09375
- w_value: bfloat16 [4096, 4096], P(None, 'head'), may hold values from -0.09375 to 0.09375
- norm_gain: float32 [4096], P('head'), may hold values from 0.25 to 1.75
- w_out: bfloat16 [4096, 4096], P('head'), may hold values from -0.125 to 0.125
Outputs:
- mixed: bfloat16 [16384, 4096], P('seq', 'head')
All inputs are finite; a program needn't handle non-finite values.
Results may differ from a plain program's by a relative error of at most 0.02.
Values may be sent and summed in bfloat16 or wider, within the bound.
No kernel may reach another device: no remote copies, remote signals or barrier semaphores. Data moves between devices by JAX's collectives and lax.ppermute only.
A program may use at most 128 MiB of HBM per device.

v0:
```python
import jax
import jax.numpy as jnp
from jax import lax
from jax.sharding import PartitionSpec as P

HEAD_DIM = 128
SPAN = 128


def prefix(shard, axis, combine, identity):
    size, index = (lax.axis_size(axis), lax.axis_index(axis))
    everything = lax.all_gather(shard.astype(jnp.bfloat16), axis)
    start = jnp.broadcast_to(jnp.asarray(identity, shard.dtype), shard.shape)

    def hop(k, before):
        reached = k < index
        new = combine(before, everything[k].astype(shard.dtype))
        return jnp.where(reached, new, before)

    return lax.fori_loop(0, size, hop, start)


def lower_mask(size):
    rows = lax.broadcasted_iota(jnp.int32, (size, size), 0)
    cols = lax.broadcasted_iota(jnp.int32, (size, size), 1)
    return (rows >= cols).astype(jnp.float32)


def add_states(earlier, later):
    return earlier + later


def local(tokens, w_query, w_key, w_value, norm_gain, w_out):
    count = tokens.shape[0]
    width = w_query.shape[1]
    heads_here = width // HEAD_DIM
    blocks = count // SPAN
    shape4 = (blocks, SPAN, heads_here, HEAD_DIM)
    q_rows = (
        jnp.dot(tokens, w_query, preferred_element_type=jnp.float32)
        .astype(jnp.bfloat16)
        .reshape(shape4)
    )
    k_rows = (
        jnp.dot(tokens, w_key, preferred_element_type=jnp.float32)
        .astype(jnp.bfloat16)
        .reshape(shape4)
    )
    v_rows = (
        jnp.dot(tokens, w_value, preferred_element_type=jnp.float32)
        .astype(jnp.bfloat16)
        .reshape(shape4)
    )
    scores = jnp.einsum("cihd,cjhd->chij", q_rows, k_rows, preferred_element_type=jnp.float32)
    scores = (scores * lower_mask(SPAN)).astype(jnp.bfloat16)
    within = jnp.einsum("chij,cjhe->cihe", scores, v_rows, preferred_element_type=jnp.float32)
    states = jnp.einsum("cjhd,cjhe->chde", k_rows, v_rows, preferred_element_type=jnp.float32)
    running = jnp.cumsum(states, axis=0)
    earlier = jnp.concatenate([jnp.zeros_like(states[:1]), running[:-1]], axis=0)
    total = running[-1]
    empty = jnp.zeros_like(total)
    carried = prefix(total, "seq", add_states, empty)
    applied = (carried[None] + earlier).astype(jnp.bfloat16)
    across = jnp.einsum("cihd,chde->cihe", q_rows, applied, preferred_element_type=jnp.float32)
    raw_out = within + across
    power = jnp.mean(raw_out * raw_out, axis=-1, keepdims=True)
    normed = raw_out * lax.rsqrt(power + 1e-06) * norm_gain.reshape(heads_here, HEAD_DIM)
    attended = normed.astype(jnp.bfloat16).reshape(count, width)
    summed = lax.psum_scatter(
        lax.dot_general(
            w_out, attended, (((0,), (1,)), ((), ())), preferred_element_type=jnp.float32
        ).astype(jnp.bfloat16),
        "head",
        scatter_dimension=0,
        tiled=True,
    ).astype(jnp.float32)
    return summed.T.astype(jnp.bfloat16)


def solution(mesh):
    in_specs = (
        P("seq", None),
        P(None, "head"),
        P(None, "head"),
        P(None, "head"),
        P("head"),
        P("head", None),
    )
    out_specs = P("seq", "head")
    return jax.shard_map(local, mesh=mesh, in_specs=in_specs, out_specs=out_specs, check_vma=False)
```

profile of v0, /device:TPU:1, one launch (start us, length us, event | category | flops | bytes accessed | tf_op | source)
XLA Modules:
  0.0 166.2 jit_solution(9983334054125854623)
XLA Ops:
  6.5 9.1 %convolution_convert_fusion = bf16[1024,512]{1,0:T(8,128)(2,1)S(1)} fusion(bf16[1024,4096]{1,0:T(8,128)(2,1)} %param.8, bf16[4096,512]{1,0:T(8,128)(2,1)} %param.10), kind=kOutput, calls=%fused_computation.10 | convolution fusion | flops 4295491584 | bytes 13631488 | tf_op jit(solution)/shard_map/dot_general | solution.py:45
  16.6 9.1 %convolution_convert_fusion.2 = bf16[1024,512]{1,0:T(8,128)(2,1)S(1)} fusion(bf16[1024,4096]{1,0:T(8,128)(2,1)} %param.8, bf16[4096,512]{1,0:T(8,128)(2,1)} %param.11), kind=kOutput, calls=%fused_computation.12 | convolution fusion | flops 4295491584 | bytes 13631488 | tf_op jit(solution)/shard_map/dot_general | solution.py:50
  26.4 2.0 %fusion.16 = f32[8,4,128,128]{3,2,1,0:T(8,128)S(1)} fusion(f32[8,4,128,128]{3,2,1,0:T(8,128)S(1)} %fusion.9), kind=kOutput, calls=%fused_computation.28 | output fusion | flops 3670016 | bytes 4194304 | tf_op jit(solution)/shard_map/jit(cumsum)/reduce_window_sum | solution.py:58
  28.4 1.3 copy-done
  30.7 3.0 %slice.10 = f32[7,4,128,128]{3,2,1,0:T(8,128)} slice(f32[8,4,128,128]{3,2,1,0:T(8,128)} %copy-done), slice={[0:7], [0:4], [0:128], [0:128]} | slice | bytes 3670016 | tf_op jit(solution)/shard_map/slice | solution.py:59
  33.7 10.0 %convolution_convert_fusion.1 = bf16[1024,512]{1,0:T(8,128)(2,1)} fusion(bf16[1024,4096]{1,0:T(8,128)(2,1)} %param.8, bf16[4096,512]{1,0:T(8,128)(2,1)} %param.9), kind=kOutput, calls=%fused_computation.11 | convolution fusion | flops 4295491584 | bytes 13631488 | tf_op jit(solution)/shard_map/dot_general | solution.py:40
  43.7 1.3 reshape.33
  45.1 2.5 %fusion.3 = f32[8,4,128,128]{3,2,1,0:T(8,128)} fusion(bf16[8,128,4,128]{1,3,2,0:T(8,128)(2,1)S(1)} %copy.21, f32[128,128]{1,0:T(8,128)S(1)} %fusion.14, bf16[8,128,4,128]{3,2,1,0:T(4,128)(2,1)S(1)} %reshape.32, bf16[8,128,4,128]{3,2,1,0:T(4,128)(2,1)S(1)} %reshape.33), kind=kOutput, calls=%fused_computation.13 | convolution fusion | flops 269484032 | bytes 5308416 | tf_op jit(solution)/shard_map/chij,cjhe->cihe/dot_general | solution.py:56
  47.5 29.7 %all-gather.2.cloned.1.call-done = bf16[16,4,128,128]{3,2,1,0:T(8,128)(2,1)} async-done(((bf16[1,4,128,128]{3,2,1,0:T(8,128)(2,1)}), bf16[16,4,128,128]{3,2,1,0:T(8,128)(2,1)}) %all-gather.2.cloned.1.call-update) | async-done | bytes 2097168 | tf_op jit(solution)/shard_map/all_gather | solution.py:12
  77.3 16.9 %while.14 = (s32[]{:T(128)}, f32[4,128,128]{2,1,0:T(8,128)S(1)}, s32[]{:T(128)}, bf16[16,4,128,128]{3,2,1,0:T(8,128)(2,1)}, s32[]{:T(128)}, /*index=5*/s32[]{:T(128)}) while((s32[]{:T(128)}, f32[4,128,128]{2,1,0:T(8,128)S(1)}, s32[]{:T(128)}, bf16[16,4,128,128]{3,2,1,0:T(8,128)(2,1)}, s32[]{:T(128)}, /*index=5*/s32[]{:T(128)}) %tuple.33), condition=%wide.region_2.3_spmd.clone, body=%wide.region_1.2_spmd.clone.sunk | while | flops 262148 | bytes 655461 | solution.py:20
  78.3 1.0 add_select_fusion.2
  80.4 1.0 add_select_fusion.2
  81.5 1.0 add_select_fusion.2
  83.6 1.0 add_select_fusion.2
  84.7 1.0 add_select_fusion.2
  86.8 1.0 add_select_fusion.2
  87.9 1.0 add_select_fusion.2
  90.0 1.0 add_select_fusion.2
  91.1 1.0 add_select_fusion.2
  93.2 1.0 add_select_fusion.2
  94.2 3.0 %fusion = (f32[8,128,4]{1,2,0:T(4,128)S(1)}, f32[8,4,128,128]{3,2,1,0:T(8,128)S(1)}) fusion(f32[8,4,128,128]{3,2,1,0:T(8,128)} %fusion.3, bf16[8,128,4,128]{3,2,1,0:T(4,128)(2,1)S(1)} %reshape.33, f32[7,4,128,128]{3,2,1,0:T(8,128)} %slice.10, f32[4,128,128]{2,1,0:T(8,128)S(1)} %get-tuple-element.84), kind=kOutput, calls=%fused_computation.4 | convolution fusion | flops 136835072 | bytes 7356416 | tf_op jit(solution)/shard_map/cihd,chde->cihe/dot_general | solution.py:64
  98.4 1.1 copy-done.2
  99.5 6.9 %convert_bitcast_fusion = bf16[4096,1024]{0,1:T(8,128)(2,1)} fusion(bf16[512,4096]{1,0:T(8,128)(2,1)S(1)} %copy-done.2, bf16[64,8,8,128]{3,2,1,0:T(8,128)(2,1)S(1)} %bitcast.35), kind=kOutput, calls=%fused_computation.1 | convolution fusion | flops 4299161600 | bytes 13631488 | tf_op jit(solution)/shard_map/dot_general | solution.py:70
  106.5 52.9 %reduce-scatter.2.cloned.1.call-done = bf16[512,1024]{0,1:T(8,128)(2,1)} async-done(((bf16[4096,1024]{0,1:T(8,128)(2,1)}), bf16[512,1024]{0,1:T(8,128)(2,1)}) %reduce-scatter.2.cloned.1.call-update) | async-done | bytes 1048592 | tf_op jit(solution)/shard_map/reduce_scatter | solution.py:69
  (24 shorter events, 10.0 us)
Async XLA Ops:
  6.5 70.7 %all-gather.2.cloned.1.call-start = ((), (), s32[]{:S(2)}) async-start(), calls=%async_computation.1 | async-start | bytes 2228224 | tf_op jit(solution)/shard_map/all_gather | solution.py:12
  28.4 1.3 copy-start
  30.5 128.9 %reduce-scatter.2.cloned.1.call-start = ((), (), s32[]{:S(2)}) async-start(), calls=%async_computation.2 | async-start | bytes 9437184 | tf_op jit(solution)/shard_map/reduce_scatter | solution.py:69
  94.2 3.1 %copy-start.1 = (f32[512]{0:T(512)S(1)}, f32[512]{0:T(512)}, u32[]{:S(2)}) copy-start(f32[512]{0:T(512)} %param.12) | copy-start | bytes 6148
  97.3 2.2 %copy-start.2 = (bf16[512,4096]{1,0:T(8,128)(2,1)S(1)}, bf16[512,4096]{1,0:T(8,128)(2,1)}, u32[]{:S(2)}) copy-start(bf16[512,4096]{1,0:T(8,128)(2,1)} %param.13) | copy-start | bytes 12582916
Sparse Core Ops, SparseCore 0:
  30.6 46.6 all-gather.1
  106.6 52.7 reduce-scatter.1
where the time goes:
time: 167 us; the launch traced here: 166 us
  waiting for transfers between devices  82.7 us (50%)
  matrix products  41 us (25%)
  other arithmetic  19 us (11%)
  between operations  13.5 us (8%)
  local copies, waits for them, and re-layouts  9.37 us (6%)
    reduce_scatter x1, waiting for transfers between devices, local(): lax.psum_scatter(lax.dot_general(w_out, attended, (((0,), (1,)), ((), ())...  52.9 us
    all_gather x1, waiting for transfers between devices, prefix(): everything = lax.all_gather(shard.astype(jnp.bfloat16), axis)  29.7 us
    select_n x16, other arithmetic, hop(): return jnp.where(reached, new, before)  16.6 us
    dot_general x1, matrix products, local(): jnp.dot(tokens, w_query, preferred_element_type=jnp.float32)  10 us
    dot_general x1, matrix products, local(): jnp.dot(tokens, w_key, preferred_element_type=jnp.float32)  9.06 us
    dot_general x1, matrix products, local(): jnp.dot(tokens, w_value, preferred_element_type=jnp.float32)  9.05 us
    dot_general x1, matrix products, local(): lax.dot_general(w_out, attended, (((0,), (1,)), ((), ())), preferred_elem...  6.92 us
  transfers between devices with their start and end apart: 2, of which 2 were waited for; matrix products, arithmetic and copies ran while one was open for 10% of the time, Pallas kernels for 0%

commit v1 on v0

v1 whole, which is shorter than its diff:
```python
import jax
import jax.numpy as jnp
from jax import lax
from jax.experimental import pallas as pl
from jax.experimental.pallas import tpu as pltpu
from jax.sharding import PartitionSpec as P


HEAD_DIM = 128
BLOCK = 256
RING = 4
F32, BF16 = jnp.float32, jnp.bfloat16
IN_VMEM = pl.BlockSpec(memory_space=pltpu.VMEM)
IN_HBM = pl.BlockSpec(memory_space=pltpu.HBM)
IN_SMEM = pl.BlockSpec(memory_space=pltpu.SMEM)


def dot(a, b):
    return jnp.dot(a, b, preferred_element_type=F32)


def dot_t(a, b, da, db):
    return lax.dot_general(a, b, (((da,), (db,)), ((), ())), preferred_element_type=F32)


def call(kernel, in_specs, out_shape, args, flops, nbytes, mib, scratch=(), aliases=None):
    return pl.pallas_call(
        kernel,
        in_specs=in_specs,
        out_specs=jax.tree.map(lambda _: IN_VMEM, out_shape),
        out_shape=out_shape,
        scratch_shapes=scratch,
        compiler_params=pltpu.CompilerParams(vmem_limit_bytes=mib * 2**20),
        cost_estimate=pl.CostEstimate(
            flops=int(flops), bytes_accessed=int(nbytes), transcendentals=0
        ),
        input_output_aliases=aliases or {},
    )(*args)


def held(x):
    return pltpu.with_memory_space_constraint(x, pltpu.VMEM)


def streamed(x):
    return pltpu.with_memory_space_constraint(x, pltpu.HBM)


SLOTS = 3


def project(tokens, weights, rows, states=False, after=(), into=None, bring=()):
    count, depth = tokens.shape
    width = weights[0].shape[1]
    first, size_m = rows.start, rows.stop - rows.start
    n_w = len(weights)
    big = depth // 4
    sizes = [big // 2, big // 2] + [big] * 3
    starts = [sum(sizes[:k]) for k in range(len(sizes))]
    steps = len(sizes)
    extra = len(after) + (into is not None)

    def kernel(*refs):
        t_hbm, w_hbm = refs[0], refs[1 : 1 + n_w]
        b_hbm = refs[1 + n_w : 1 + n_w + len(bring)]
        rest = refs[1 + n_w + len(bring) + extra :]
        outs, rest = rest[:n_w], rest[n_w:]
        if states:
            s_ref, rest = rest[0], rest[1:]
        if bring:
            b_ref, rest = rest[0], rest[1:]
        t_buf, w_buf, acc, t_sem, w_sem = rest[:5]

        def copies(k):
            at, size, slot = pl.ds(starts[k], sizes[k]), pl.ds(0, sizes[k]), k % SLOTS
            moves = [
                pltpu.make_async_copy(
                    t_hbm.at[pl.ds(first, size_m), at], t_buf.at[slot, :, size], t_sem.at[k]
                )
            ]
            for i in range(n_w):
                moves.append(
                    pltpu.make_async_copy(
                        w_hbm[i].at[at, :], w_buf.at[slot, i, size, :], w_sem.at[k, i]
                    )
                )
            return moves

        brought = [
            pltpu.make_async_copy(
                source, b_ref.at[pl.ds(i * source.shape[0], source.shape[0]), :], rest[5].at[i]
            )
            for i, source in enumerate(b_hbm)
        ]
        for k in range(SLOTS - 1):
            for move in copies(k):
                move.start()
        for k in range(steps):
            for move in copies(k):
                move.wait()
            if k + SLOTS - 1 < steps:
                for move in copies(k + SLOTS - 1):
                    move.start()
            if k + SLOTS == steps:
                for move in brought:
                    move.start()
            slot, size = k % SLOTS, sizes[k]
            for i in range(n_w):
                product = dot(t_buf[slot, :, :size], w_buf[slot, i, :size, :])
                if k == 0:
                    acc[i] = product
                elif k < steps - 1:
                    acc[i] += product
                else:
                    outs[i][first : first + size_m, :] = (acc[i] + product).astype(BF16)
        if states:
            for h in range(width // HEAD_DIM):
                cols = slice(h * HEAD_DIM, (h + 1) * HEAD_DIM)
                s_ref[cols, :] = dot_t(outs[0][:, cols], outs[1][:, cols], 0, 0).astype(BF16)
        for move in brought:
            move.wait()

    out_shape = [pltpu.VMEM((count, width), BF16)] * n_w
    scratch = [
        pltpu.VMEM((SLOTS, size_m, big), BF16),
        pltpu.VMEM((SLOTS, n_w, big, width), BF16),
        pltpu.VMEM((n_w, size_m, width), F32),
        pltpu.SemaphoreType.DMA((steps,)),
        pltpu.SemaphoreType.DMA((steps, n_w)),
    ]
    if states:
        out_shape = out_shape + [pltpu.VMEM((width, HEAD_DIM), BF16)]
    if bring:
        tall = sum(b.shape[0] for b in bring)
        out_shape = out_shape + [pltpu.VMEM((tall, bring[0].shape[1]), BF16)]
        scratch = scratch + [pltpu.SemaphoreType.DMA((len(bring),))]
    in_specs = [IN_HBM] * (1 + n_w + len(bring)) + [pl.BlockSpec(memory_space=pl.ANY)] * len(after)
    args = (streamed(tokens), *map(streamed, weights), *map(streamed, bring), *after)
    aliases = None
    if into is not None:
        aliases = {len(args): 0}
        in_specs, args = in_specs + [IN_VMEM], (*args, into)
    return call(
        kernel,
        in_specs,
        out_shape,
        args,
        2 * size_m * depth * width * n_w,
        2 * depth * (size_m + width * n_w),
        28,
        scratch,
        aliases,
    )


def row_total(total, came, after):
    def kernel(*refs):
        refs[-1][...] = sum((r[...].astype(F32) for r in refs[1:-2]), refs[0][...].astype(F32)).astype(
            BF16
        )

    return call(
        kernel,
        [IN_VMEM] * (1 + len(came)) + [pl.BlockSpec(memory_space=pl.ANY)],
        pltpu.VMEM(total.shape, BF16),
        (total, *came, after),
        4 * total.size,
        8 * total.size,
        4,
    )


def local_attention(q, k, v):
    count, width = q.shape
    heads = width // HEAD_DIM
    blocks = count // BLOCK

    def kernel(q_ref, k_ref, v_ref, w_ref, e_ref):
        rows = lax.broadcasted_iota(jnp.int32, (BLOCK, BLOCK), 0)
        cols = lax.broadcasted_iota(jnp.int32, (BLOCK, BLOCK), 1)
        keep = rows >= cols
        for h in range(heads):
            at_h = slice(h * HEAD_DIM, (h + 1) * HEAD_DIM)
            state = jnp.zeros((HEAD_DIM, HEAD_DIM), F32)
            for b in range(blocks):
                at = slice(b * BLOCK, (b + 1) * BLOCK)
                kb, vb = k_ref[at, at_h], v_ref[at, at_h]
                scores = jnp.where(keep, dot_t(q_ref[at, at_h], kb, 1, 1), 0.0).astype(BF16)
                w_ref[at, at_h] = dot(scores, vb)
                e_ref[b, at_h, :] = state
                if b < blocks - 1:
                    state = state + dot_t(kb, vb, 0, 0)

    return call(
        kernel,
        [IN_VMEM] * 3,
        [pltpu.VMEM((count, width), F32), pltpu.VMEM((blocks, width, HEAD_DIM), F32)],
        (q, k, v),
        4 * count * width * (BLOCK + HEAD_DIM),
        14 * count * width,
        8,
    )


def attend(place, index, q, within, earlier, from_x, from_z, gain, mine, block, after=()):
    count, width = q.shape
    heads = width // HEAD_DIM
    per_half = count // BLOCK // 2
    hops = len(SHIFTS)

    def kernel(place_ref, index_ref, q_ref, w_ref, e_ref, *refs):
        xs, zs, g_ref, o_ref = refs[:hops], refs[hops : 2 * hops], refs[2 * hops], refs[-1]
        half = place_ref[0] % 2 if mine else 1 - place_ref[0] % 2
        at_x, at_z = index_ref[0] % RING, index_ref[0] // RING
        here = half * per_half + block
        rows = pl.ds(pl.multiple_of(here * BLOCK, BLOCK), BLOCK)
        for h in range(heads):
            cols = slice(h * HEAD_DIM, (h + 1) * HEAD_DIM)
            state = e_ref[here, cols, :]
            for at, came in ((at_x, xs), (at_z, zs)):
                for shift, ref in zip(SHIFTS, came):
                    source = (at - shift + RING) % RING
                    state += jnp.where(source < at, ref[cols, :].astype(F32), 0.0)
            raw = w_ref[rows, cols] + dot(q_ref[rows, cols], state.astype(BF16))
            power = jnp.mean(raw * raw, axis=-1, keepdims=True)
            o_ref[:, cols] = (raw * lax.rsqrt(power + 1e-06) * g_ref[:, cols]).astype(BF16)

    return call(
        kernel,
        [IN_SMEM] * 2
        + [IN_VMEM] * (4 + 2 * hops)
        + [pl.BlockSpec(memory_space=pl.ANY)] * len(after),
        pltpu.VMEM((BLOCK, width), BF16),
        (place, index, q, within, earlier, *from_x, *from_z, gain, *after),
        count * width * HEAD_DIM // 2,
        2 * count * width,
        8,
    )


def out_project(place, mine, theirs, w_out, pieces, form, added=(), after=()):
    size, width = mine[0].shape
    n_p = len(pieces)

    def kernel(place_ref, *refs):
        xs, ys, w_ref = refs[:2], refs[2:4], refs[4]
        adds, outs = refs[5 : 5 + len(added)], refs[5 + len(added) + len(after) :]
        y, c = place_ref[0] // 2, place_ref[0] % 2
        for p, (block, step) in enumerate(pieces):
            chip = (y + step + RING) % RING
            for side in range(2):
                core = c if side == 0 else 1 - c
                cols = pl.ds(pl.multiple_of((chip * 2 + core) * width, width), width)
                total = dot(xs[block][...], w_ref[:width, cols])
                total = total + dot(ys[block][...], w_ref[width:, cols])
                here = slice(side * width, (side + 1) * width)
                if added:
                    total = total + adds[p][:, here].astype(F32)
                total = total.astype(BF16)
                if form == "joined":
                    outs[p][:, here] = total
                elif form == "apart":
                    outs[2 * p + side][...] = total
                else:
                    outs[side][p * size : (p + 1) * size, :] = total

    if form == "joined":
        out_shape = [pltpu.VMEM((size, 2 * width), BF16)] * n_p
    elif form == "apart":
        out_shape = [pltpu.VMEM((size, width), BF16)] * (2 * n_p)
    else:
        out_shape = [pltpu.VMEM((n_p * size, width), BF16)] * 2
    return call(
        kernel,
        [IN_SMEM]
        + [IN_VMEM] * (5 + len(added))
        + [pl.BlockSpec(memory_space=pl.ANY)] * len(after),
        out_shape,
        (place, *mine, *theirs, w_out, *added, *after),
        8 * n_p * size * width * width,
        8 * width * width,
        12,
    )


def final_sum(place, own, own_cross, near, late, count):
    size, width = near[0][0].shape

    def kernel(place_ref, own_ref, cross_ref, *refs):
        o_ref = refs[-1]
        c = place_ref[0] % 2
        for which, base in enumerate((own_ref, cross_ref)):
            half = c if which == 0 else 1 - c
            for b in range(2):
                at = slice(b * size, (b + 1) * size)
                total = base[at, :].astype(F32)
                total = total + refs[2 * b + which][...].astype(F32)
                total = total + refs[4 + 2 * b + which][...].astype(F32)
                start = pl.multiple_of(half * (2 * size) + b * size, size)
                o_ref[pl.ds(start, size), :] = total.astype(BF16)

    terms = [a for pair in near for a in pair] + [a for pair in late for a in pair]
    return call(
        kernel,
        [IN_SMEM] + [IN_VMEM] * (2 + len(terms)),
        jax.ShapeDtypeStruct((count, width), BF16),
        (place, own, own_cross, *terms),
        12 * size * width,
        24 * size * width,
        8,
    )


SHIFTS = (1, -1, 2)


def head_send(x, step, cross=0):
    pairs = [
        (h, ((h // 2 + step) % RING) * 2 + ((h % 2) ^ cross)) for h in range(2 * RING)
    ]
    return held(lax.ppermute(x, "head", pairs))


def seq_send(x, dz, dx):
    pairs = [
        (s, ((s // RING + dz) % RING) * RING + (s % RING + dx) % RING) for s in range(RING * RING)
    ]
    return held(lax.ppermute(x, "seq", pairs))


def local(tokens, w_query, w_key, w_value, norm_gain, w_out):
    count = tokens.shape[0]
    place = lax.axis_index("head").astype(jnp.int32).reshape(1)
    index = lax.axis_index("seq").astype(jnp.int32).reshape(1)

    w_theirs = lax.ppermute(w_out, "head", [(h, h ^ 1) for h in range(2 * RING)])
    keys, values, total = project(tokens, [w_key, w_value], slice(0, count), states=True)
    from_x = [seq_send(total, 0, d) for d in SHIFTS]
    cut = count - BLOCK
    queries, w_held = project(
        tokens, [w_query], slice(0, cut), after=(total,), bring=(w_out, w_theirs)
    )
    row = row_total(total, from_x, queries)
    from_z = [seq_send(row, d, 0) for d in SHIFTS]
    (queries,) = project(tokens, [w_query], slice(cut, count), after=(row,), into=queries)
    within, earlier = local_attention(queries, keys, values)

    def attended(mine, block, **kw):
        gain = norm_gain.reshape(1, -1)
        return attend(
            place, index, queries, within, earlier, from_x, from_z, gain, mine, block, **kw
        )

    def project_out(pieces, form, blocks=(0, 1), **kw):
        x, y = [mine[b] for b in blocks], [theirs[b] for b in blocks]
        return out_project(place, x, y, w_held, pieces, form, **kw)

    other0 = attended(False, 0)
    other1 = attended(False, 1, after=(other0,))
    theirs = [head_send(other0, 0, 1), head_send(other1, 0, 1)]
    mine = [attended(True, 0, after=(other1,))]
    (far0,) = project_out([(0, 2)], "joined", blocks=(0, 0))
    mine.append(attended(True, 1, after=(far0,)))
    (far1,) = project_out([(0, 2)], "joined", blocks=(1, 1))
    near = project_out([(0, 1), (1, -1)], "apart", after=(far1,))
    far0, far1 = head_send(far0, -1), head_send(far1, 1)

    def last_hop(up_s, up_x, down_s, down_x):
        up, down = head_send(up_s, 1), head_send(down_s, -1)
        up_x = head_send(up_x, 1, 1)
        return (up, up_x), (down, head_send(down_x, -1, 1))

    own, own_cross = project_out([(0, 0), (1, 0)], "stacked", after=(near[0],))
    near = last_hop(*near)
    own_cross = head_send(own_cross, 0, 1)
    late = project_out([(1, 1), (0, -1)], "apart", added=(far1, far0))
    late = last_hop(*late)[::-1]
    return final_sum(place, own, own_cross, near, late, count)


def solution(mesh):
    in_specs = (
        P("seq", None),
        P(None, "head"),
        P(None, "head"),
        P(None, "head"),
        P("head"),
        P("head", None),
    )
    out_specs = P("seq", "head")
    return jax.shard_map(local, mesh=mesh, in_specs=in_specs, out_specs=out_specs, check_vma=False)
```

time: 167 us -> 87 us (0.52)
  waiting for transfers between devices: 82.7 us -> 26.2 us
  matrix products: 41 us -> 0 us
  Pallas kernels: 0 us -> 35.3 us
  starting transfers between devices: 0.22 us -> 25.1 us
  other arithmetic: 19 us -> 0 us
  between operations: 13.5 us -> 0.2 us
  local copies, waits for them, and re-layouts: 9.37 us -> 0.01 us
    reduce_scatter x1 -> x0, waiting for transfers between devices: 52.9 us -> none  [local(): lax.psum_scatter(lax.dot_general(w_out, attended, (((0,), (1,)), ((), ())...]
    dot_general x7 -> x0, matrix products: 41 us -> none  [the longest x1 10 us: local(): jnp.dot(tokens, w_query, preferred_element_type=jnp.float32)]
    pallas_call x0 -> x15, Pallas kernels: none -> 35.3 us  [call(): pl.pallas_call(kernel, in_specs=in_specs, out_specs=jax.tree.map(lambda _...]
    all_gather x1 -> x0, waiting for transfers between devices: 29.7 us -> none  [prefix(): everything = lax.all_gather(shard.astype(jnp.bfloat16), axis)]
    ppermute x0 -> x20, waiting for transfers between devices: none -> 26.2 us  [the longest x13 26.2 us: head_send(): return held(lax.ppermute(x, 'head', pairs))]
    ppermute x0 -> x20, starting transfers between devices: none -> 25.1 us  [the longest x13 14.1 us: head_send(): return held(lax.ppermute(x, 'head', pairs))]
    select_n x16 -> x0, other arithmetic: 16.6 us -> none  [hop(): return jnp.where(reached, new, before)]
    slice x2 -> x0, local copies, waits for them, and re-layouts: 3.67 us -> none  [the longest x1 2.97 us: local(): running[:-1]]
  transfers between devices with their start and end apart: 2 -> 20, of which waited for: 2 -> 8; matrix products, arithmetic and copies ran while one was open for 10% -> 0% of each run, Pallas kernels for 0% -> 38%
where the time goes in v1:
time: 87 us; the launch traced here: 86.8 us
  Pallas kernels  35.3 us (41%)
  waiting for transfers between devices  26.2 us (30%)
  starting transfers between devices  25.1 us (29%)
    pallas_call x15, Pallas kernels, call(): pl.pallas_call(kernel, in_specs=in_specs, out_specs=jax.tree.map(lambda _...  35.3 us
    ppermute x13, waiting for transfers between devices, head_send(): return held(lax.ppermute(x, 'head', pairs))  26.2 us
    ppermute x13, starting transfers between devices, head_send(): return held(lax.ppermute(x, 'head', pairs))  14.1 us
    ppermute x6, starting transfers between devices, seq_send(): return held(lax.ppermute(x, 'seq', pairs))  9.53 us
  transfers between devices with their start and end apart: 20, of which 8 were waited for; matrix products, arithmetic and copies ran while one was open for 0% of the time, Pallas kernels for 38%

profile of v1, /device:TPU:1, one launch (start us, length us, event | category | flops | bytes accessed | tf_op | source)
XLA Modules:
  0.0 86.8 jit_solution(7717843784591667878)
XLA Ops:
  0.0 1.4 %collective-permute-start.3 = (bf16[512,4096]{1,0:T(8,128)(2,1)}, bf16[512,4096]{1,0:T(8,128)(2,1)}, u32[]{:S(2)}, u32[]{:S(2)}) collective-permute-start(bf16[512,4096]{1,0:T(8,128)(2,1)} %refs_2_.3), channel_id=1, source_target_pairs={{0,1},{1,0},{2,3},{3,2},{4,5},{5,4},{6,7},{7,6},{8,9},{9,8},{10,11... | collective-permute-start | bytes 12582920 | tf_op jit(solution)/shard_map/ppermute | solution.py:336
  1.4 11.9 %shard_map.64 = (bf16[1024,512]{1,0:T(8,128)(2,1)S(1)}, bf16[1024,512]{1,0:T(8,128)(2,1)S(1)}, bf16[512,128]{1,0:T(8,128)(2,1)S(1)}) custom-call(bf16[1024,4096]{1,0:T(8,128)(2,1)} %refs_0_.5, bf16[4096,512]{1,0:T(8,128)(2,1)} %refs_1_.3, bf16[4096,512]{1,0:T(8,128)(2,1)} %refs_2_.2), custom_call_target="tpu_custom_call" | custom-call | flops 8589934592 | bytes 16777216 | tf_op jit(solution)/shard_map/pallas_call | solution.py:27
  13.3 1.4 %collective-permute-start = (bf16[512,128]{1,0:T(8,128)(2,1)S(1)}, bf16[512,128]{1,0:T(8,128)(2,1)S(1)}, u32[]{:S(2)}, u32[]{:S(2)}) collective-permute-start(bf16[512,128]{1,0:T(8,128)(2,1)S(1)} %get-tuple-element.22.refs_4_.refs_0_), channel_id=1, source_target_pairs={{0,8},{8,16},{16,24},{24,0},{32,40},{40,48},{48,56},{56,32},{64,72... | collective-permute-start | bytes 393224 | tf_op jit(solution)/shard_map/ppermute | solution.py:328
  14.7 1.3 %collective-permute-start.1 = (bf16[512,128]{1,0:T(8,128)(2,1)S(1)}, bf16[512,128]{1,0:T(8,128)(2,1)S(1)}, u32[]{:S(2)}, u32[]{:S(2)}) collective-permute-start(bf16[512,128]{1,0:T(8,128)(2,1)S(1)} %get-tuple-element.22.refs_4_.refs_0_), channel_id=1, source_target_pairs={{0,24},{8,0},{16,8},{24,16},{32,56},{40,32},{48,40},{56,48},{64,88... | collective-permute-start | bytes 393224 | tf_op jit(solution)/shard_map/ppermute | solution.py:328
  16.1 1.6 %collective-permute-start.2 = (bf16[512,128]{1,0:T(8,128)(2,1)S(1)}, bf16[512,128]{1,0:T(8,128)(2,1)S(1)}, u32[]{:S(2)}, u32[]{:S(2)}) collective-permute-start(bf16[512,128]{1,0:T(8,128)(2,1)S(1)} %get-tuple-element.22.refs_4_.refs_0_), channel_id=1, source_target_pairs={{0,16},{8,24},{16,0},{24,8},{32,48},{40,56},{48,32},{56,40},{64,80... | collective-permute-start | bytes 393224 | tf_op jit(solution)/shard_map/ppermute | solution.py:328
  17.7 7.6 %shard_map.65 = (bf16[1024,512]{1,0:T(8,128)(2,1)S(1)}, bf16[1024,4096]{1,0:T(8,128)(2,1)S(1)}) custom-call(bf16[1024,4096]{1,0:T(8,128)(2,1)} %refs_0_.5, bf16[4096,512]{1,0:T(8,128)(2,1)} %refs_1_.5, bf16[512,4096]{1,0:T(8,128)(2,1)} %refs_2_.3, bf16[512,4096]{1,0:T(8,128)(2,1)} %collective-permute-done.3.refs_3_, ...), custom_call_target="tpu_custom_call" | custom-call | flops 3221225472 | bytes 10485760 | tf_op jit(solution)/shard_map/pallas_call | solution.py:27
  25.4 1.7 %collective-permute-start.4 = (bf16[512,128]{1,0:T(8,128)(2,1)S(1)}, bf16[512,128]{1,0:T(8,128)(2,1)S(1)}, u32[]{:S(2)}, u32[]{:S(2)}) collective-permute-start(bf16[512,128]{1,0:T(8,128)(2,1)S(1)} %shard_map.66.refs_2_), channel_id=1, source_target_pairs={{0,32},{8,40},{16,48},{24,56},{32,64},{40,72},{48,80},{56,88},{64,... | collective-permute-start | bytes 393224 | tf_op jit(solution)/shard_map/ppermute | solution.py:328
  27.1 2.2 %collective-permute-start.5 = (bf16[512,128]{1,0:T(8,128)(2,1)S(1)}, bf16[512,128]{1,0:T(8,128)(2,1)S(1)}, u32[]{:S(2)}, u32[]{:S(2)}) collective-permute-start(bf16[512,128]{1,0:T(8,128)(2,1)S(1)} %shard_map.66.refs_2_), channel_id=1, source_target_pairs={{0,96},{8,104},{16,112},{24,120},{32,0},{40,8},{48,16},{56,24},{64... | collective-permute-start | bytes 393224 | tf_op jit(solution)/shard_map/ppermute | solution.py:328
  30.5 4.5 %shard_map.67.q_ref = bf16[1024,512]{1,0:T(8,128)(2,1)S(1)} custom-call(bf16[1024,4096]{1,0:T(8,128)(2,1)} %refs_0_.5, bf16[4096,512]{1,0:T(8,128)(2,1)} %refs_1_.5, bf16[512,128]{1,0:T(8,128)(2,1)S(1)} %shard_map.66.refs_2_, bf16[1024,512]{1,0:T(8,128)(2,1)S(1)} %get-tuple-element.23.refs_4_.refs_3_), custom_call_target="tpu_custom_call", output_to_operand_aliasing={{}: (3, {})} | custom-call | flops 1073741824 | bytes 6291456 | tf_op jit(solution)/shard_map/pallas_call | solution.py:27
  35.1 2.7 %shard_map.68 = (f32[1024,512]{1,0:T(8,128)S(1)}, f32[4,512,128]{2,1,0:T(8,128)S(1)}) custom-call(bf16[1024,512]{1,0:T(8,128)(2,1)S(1)} %shard_map.67.q_ref, bf16[1024,512]{1,0:T(8,128)(2,1)S(1)} %get-tuple-element.24.k_ref, bf16[1024,512]{1,0:T(8,128)(2,1)S(1)} %get-tuple-element.25.v_ref), custom_call_target="tpu_custom_call" | custom-call | flops 805306368 | bytes 7340032 | tf_op jit(solution)/shard_map/pallas_call | solution.py:27
  38.3 1.8 %collective-permute-start.7 = (bf16[256,512]{1,0:T(8,128)(2,1)S(1)}, bf16[256,512]{1,0:T(8,128)(2,1)S(1)}, u32[]{:S(2)}, u32[]{:S(2)}) collective-permute-start(bf16[256,512]{1,0:T(8,128)(2,1)S(1)} %shard_map.69.refs_7_), channel_id=1, source_target_pairs={{0,1},{1,0},{2,3},{3,2},{4,5},{5,4},{6,7},{7,6},{8,9},{9,8},{10,11... | collective-permute-start | bytes 786440 | tf_op jit(solution)/shard_map/ppermute | solution.py:321
  43.2 1.4 %collective-permute-start.14 = (bf16[256,1024]{1,0:T(8,128)(2,1)S(1)}, bf16[256,1024]{1,0:T(8,128)(2,1)S(1)}, u32[]{:S(2)}, u32[]{:S(2)}) collective-permute-start(bf16[256,1024]{1,0:T(8,128)(2,1)S(1)} %shard_map.74.refs_5_), channel_id=1, source_target_pairs={{0,2},{1,3},{2,4},{3,5},{4,6},{5,7},{6,0},{7,1},{8,10},{9,11},{10,... | collective-permute-start | bytes 1572872 | tf_op jit(solution)/shard_map/ppermute | solution.py:321
  44.6 1.5 %collective-permute-start.15 = (bf16[256,1024]{1,0:T(8,128)(2,1)S(1)}, bf16[256,1024]{1,0:T(8,128)(2,1)S(1)}, u32[]{:S(2)}, u32[]{:S(2)}) collective-permute-start(bf16[256,1024]{1,0:T(8,128)(2,1)S(1)} %shard_map.72.refs_7_), channel_id=1, source_target_pairs={{0,6},{1,7},{2,0},{3,1},{4,2},{5,3},{6,4},{7,5},{8,14},{9,15},{10,... | collective-permute-start | bytes 1572872 | tf_op jit(solution)/shard_map/ppermute | solution.py:321
  50.0 1.3 %collective-permute-start.11 = (bf16[256,512]{1,0:T(8,128)(2,1)S(1)}, bf16[256,512]{1,0:T(8,128)(2,1)S(1)}, u32[]{:S(2)}, u32[]{:S(2)}) collective-permute-start(bf16[256,512]{1,0:T(8,128)(2,1)S(1)} %get-tuple-element.32), channel_id=1, source_target_pairs={{0,3},{1,2},{2,5},{3,4},{4,7},{5,6},{6,1},{7,0},{8,11},{9,10},{10,... | collective-permute-start | bytes 786440 | tf_op jit(solution)/shard_map/ppermute | solution.py:321
  51.3 6.4 %collective-permute-done.14.refs_5_ = bf16[256,1024]{1,0:T(8,128)(2,1)S(1)} collective-permute-done((bf16[256,1024]{1,0:T(8,128)(2,1)S(1)}, bf16[256,1024]{1,0:T(8,128)(2,1)S(1)}, u32[]{:S(2)}, u32[]{:S(2)}) %collective-permute-start.14) | collective-permute-done | bytes 524320 | tf_op jit(solution)/shard_map/ppermute | solution.py:321
  57.7 1.4 %collective-permute-start.12 = (bf16[256,512]{1,0:T(8,128)(2,1)S(1)}, bf16[256,512]{1,0:T(8,128)(2,1)S(1)}, u32[]{:S(2)}, u32[]{:S(2)}) collective-permute-start(bf16[256,512]{1,0:T(8,128)(2,1)S(1)} %get-tuple-element.33), channel_id=1, source_target_pairs={{0,6},{1,7},{2,0},{3,1},{4,2},{5,3},{6,4},{7,5},{8,14},{9,15},{10,... | collective-permute-start | bytes 786440 | tf_op jit(solution)/shard_map/ppermute | solution.py:321
  59.1 2.8 %collective-permute-start.13 = (bf16[256,512]{1,0:T(8,128)(2,1)S(1)}, bf16[256,512]{1,0:T(8,128)(2,1)S(1)}, u32[]{:S(2)}, u32[]{:S(2)}) collective-permute-start(bf16[256,512]{1,0:T(8,128)(2,1)S(1)} %get-tuple-element.34), channel_id=1, source_target_pairs={{0,7},{1,6},{2,1},{3,0},{4,3},{5,2},{6,5},{7,4},{8,15},{9,14},{10,... | collective-permute-start | bytes 786440 | tf_op jit(solution)/shard_map/ppermute | solution.py:321
  63.3 1.4 %collective-permute-start.16 = (bf16[256,512]{1,0:T(8,128)(2,1)S(1)}, bf16[256,512]{1,0:T(8,128)(2,1)S(1)}, u32[]{:S(2)}, u32[]{:S(2)}) collective-permute-start(bf16[256,512]{1,0:T(8,128)(2,1)S(1)} %get-tuple-element.35), channel_id=1, source_target_pairs={{0,6},{1,7},{2,0},{3,1},{4,2},{5,3},{6,4},{7,5},{8,14},{9,15},{10,... | collective-permute-start | bytes 786440 | tf_op jit(solution)/shard_map/ppermute | solution.py:321
  64.7 4.7 %collective-permute-done.11.refs_1_ = bf16[256,512]{1,0:T(8,128)(2,1)S(1)} collective-permute-done((bf16[256,512]{1,0:T(8,128)(2,1)S(1)}, bf16[256,512]{1,0:T(8,128)(2,1)S(1)}, u32[]{:S(2)}, u32[]{:S(2)}) %collective-permute-start.11) | collective-permute-done | bytes 262176 | tf_op jit(solution)/shard_map/ppermute | solution.py:321
  70.7 2.6 %collective-permute-done.13.refs_3_ = bf16[256,512]{1,0:T(8,128)(2,1)S(1)} collective-permute-done((bf16[256,512]{1,0:T(8,128)(2,1)S(1)}, bf16[256,512]{1,0:T(8,128)(2,1)S(1)}, u32[]{:S(2)}, u32[]{:S(2)}) %collective-permute-start.13) | collective-permute-done | bytes 262176 | tf_op jit(solution)/shard_map/ppermute | solution.py:321
  73.2 2.1 %collective-permute-done.16.refs_4_ = bf16[256,512]{1,0:T(8,128)(2,1)S(1)} collective-permute-done((bf16[256,512]{1,0:T(8,128)(2,1)S(1)}, bf16[256,512]{1,0:T(8,128)(2,1)S(1)}, u32[]{:S(2)}, u32[]{:S(2)}) %collective-permute-start.16) | collective-permute-done | bytes 262176 | tf_op jit(solution)/shard_map/ppermute | solution.py:321
  75.3 7.5 %collective-permute-done.17.refs_5_ = bf16[256,512]{1,0:T(8,128)(2,1)S(1)} collective-permute-done((bf16[256,512]{1,0:T(8,128)(2,1)S(1)}, bf16[256,512]{1,0:T(8,128)(2,1)S(1)}, u32[]{:S(2)}, u32[]{:S(2)}) %collective-permute-start.17) | collective-permute-done | bytes 262176 | tf_op jit(solution)/shard_map/ppermute | solution.py:321
  82.9 2.6 %collective-permute-done.19.refs_7_ = bf16[256,512]{1,0:T(8,128)(2,1)S(1)} collective-permute-done((bf16[256,512]{1,0:T(8,128)(2,1)S(1)}, bf16[256,512]{1,0:T(8,128)(2,1)S(1)}, u32[]{:S(2)}, u32[]{:S(2)}) %collective-permute-start.19) | collective-permute-done | bytes 262176 | tf_op jit(solution)/shard_map/ppermute | solution.py:321
  85.5 1.3 %shard_map.78 = bf16[1024,512]{1,0:T(8,128)(2,1)} custom-call(s32[1]{0:T(128)} %bitcast.place_ref, bf16[512,512]{1,0:T(8,128)(2,1)S(1)} %get-tuple-element.30.own_ref, bf16[512,512]{1,0:T(8,128)(2,1)S(1)} %collective-permute-done.9.cross_ref, bf16[256,512]{1,0:T(8,128)(2,1)S(1)} %collective-permute-done.10.refs_0_, ...), custom_call_target="tpu_custom_call" | custom-call | flops 1572864 | bytes 3145728 | tf_op jit(solution)/shard_map/pallas_call | solution.py:27
  (33 shorter events, 11.4 us)
Async XLA Ops:
  0.0 17.7 %collective-permute-start.3 = (bf16[512,4096]{1,0:T(8,128)(2,1)}, bf16[512,4096]{1,0:T(8,128)(2,1)}, u32[]{:S(2)}, u32[]{:S(2)}) collective-permute-start(bf16[512,4096]{1,0:T(8,128)(2,1)} %refs_2_.3), channel_id=1, source_target_pairs={{0,1},{1,0},{2,3},{3,2},{4,5},{5,4},{6,7},{7,6},{8,9},{9,8},{10,11... | collective-permute-start | bytes 12582920 | tf_op jit(solution)/shard_map/ppermute | solution.py:336
  13.3 12.0 %collective-permute-start = (bf16[512,128]{1,0:T(8,128)(2,1)S(1)}, bf16[512,128]{1,0:T(8,128)(2,1)S(1)}, u32[]{:S(2)}, u32[]{:S(2)}) collective-permute-start(bf16[512,128]{1,0:T(8,128)(2,1)S(1)} %get-tuple-element.22.refs_4_.refs_0_), channel_id=1, source_target_pairs={{0,8},{8,16},{16,24},{24,0},{32,40},{40,48},{48,56},{56,32},{64,72... | collective-permute-start | bytes 393224 | tf_op jit(solution)/shard_map/ppermute | solution.py:328
  14.7 10.6 %collective-permute-start.1 = (bf16[512,128]{1,0:T(8,128)(2,1)S(1)}, bf16[512,128]{1,0:T(8,128)(2,1)S(1)}, u32[]{:S(2)}, u32[]{:S(2)}) collective-permute-start(bf16[512,128]{1,0:T(8,128)(2,1)S(1)} %get-tuple-element.22.refs_4_.refs_0_), channel_id=1, source_target_pairs={{0,24},{8,0},{16,8},{24,16},{32,56},{40,32},{48,40},{56,48},{64,88... | collective-permute-start | bytes 393224 | tf_op jit(solution)/shard_map/ppermute | solution.py:328
  16.1 9.2 %collective-permute-start.2 = (bf16[512,128]{1,0:T(8,128)(2,1)S(1)}, bf16[512,128]{1,0:T(8,128)(2,1)S(1)}, u32[]{:S(2)}, u32[]{:S(2)}) collective-permute-start(bf16[512,128]{1,0:T(8,128)(2,1)S(1)} %get-tuple-element.22.refs_4_.refs_0_), channel_id=1, source_target_pairs={{0,16},{8,24},{16,0},{24,8},{32,48},{40,56},{48,32},{56,40},{64,80... | collective-permute-start | bytes 393224 | tf_op jit(solution)/shard_map/ppermute | solution.py:328
  25.4 12.4 %copy-start = (f32[512]{0:T(512)S(1)}, f32[512]{0:T(512)}, u32[]{:S(2)}) copy-start(f32[512]{0:T(512)} %param.10) | copy-start | bytes 6148
  25.4 12.4 %collective-permute-start.4 = (bf16[512,128]{1,0:T(8,128)(2,1)S(1)}, bf16[512,128]{1,0:T(8,128)(2,1)S(1)}, u32[]{:S(2)}, u32[]{:S(2)}) collective-permute-start(bf16[512,128]{1,0:T(8,128)(2,1)S(1)} %shard_map.66.refs_2_), channel_id=1, source_target_pairs={{0,32},{8,40},{16,48},{24,56},{32,64},{40,72},{48,80},{56,88},{64,... | collective-permute-start | bytes 393224 | tf_op jit(solution)/shard_map/ppermute | solution.py:328
  27.1 10.7 %collective-permute-start.5 = (bf16[512,128]{1,0:T(8,128)(2,1)S(1)}, bf16[512,128]{1,0:T(8,128)(2,1)S(1)}, u32[]{:S(2)}, u32[]{:S(2)}) collective-permute-start(bf16[512,128]{1,0:T(8,128)(2,1)S(1)} %shard_map.66.refs_2_), channel_id=1, source_target_pairs={{0,96},{8,104},{16,112},{24,120},{32,0},{40,8},{48,16},{56,24},{64... | collective-permute-start | bytes 393224 | tf_op jit(solution)/shard_map/ppermute | solution.py:328
  29.3 8.5 %collective-permute-start.6 = (bf16[512,128]{1,0:T(8,128)(2,1)S(1)}, bf16[512,128]{1,0:T(8,128)(2,1)S(1)}, u32[]{:S(2)}, u32[]{:S(2)}) collective-permute-start(bf16[512,128]{1,0:T(8,128)(2,1)S(1)} %shard_map.66.refs_2_), channel_id=1, source_target_pairs={{0,64},{8,72},{16,80},{24,88},{32,96},{40,104},{48,112},{56,120},{... | collective-permute-start | bytes 393224 | tf_op jit(solution)/shard_map/ppermute | solution.py:328
  38.3 2.9 %collective-permute-start.7 = (bf16[256,512]{1,0:T(8,128)(2,1)S(1)}, bf16[256,512]{1,0:T(8,128)(2,1)S(1)}, u32[]{:S(2)}, u32[]{:S(2)}) collective-permute-start(bf16[256,512]{1,0:T(8,128)(2,1)S(1)} %shard_map.69.refs_7_), channel_id=1, source_target_pairs={{0,1},{1,0},{2,3},{3,2},{4,5},{5,4},{6,7},{7,6},{8,9},{9,8},{10,11... | collective-permute-start | bytes 786440 | tf_op jit(solution)/shard_map/ppermute | solution.py:321
  40.6 1.9 %collective-permute-start.8 = (bf16[256,512]{1,0:T(8,128)(2,1)S(1)}, bf16[256,512]{1,0:T(8,128)(2,1)S(1)}, u32[]{:S(2)}, u32[]{:S(2)}) collective-permute-start(bf16[256,512]{1,0:T(8,128)(2,1)S(1)} %shard_map.70.refs_7_), channel_id=1, source_target_pairs={{0,1},{1,0},{2,3},{3,2},{4,5},{5,4},{6,7},{7,6},{8,9},{9,8},{10,11... | collective-permute-start | bytes 786440 | tf_op jit(solution)/shard_map/ppermute | solution.py:321
  43.2 14.5 %collective-permute-start.14 = (bf16[256,1024]{1,0:T(8,128)(2,1)S(1)}, bf16[256,1024]{1,0:T(8,128)(2,1)S(1)}, u32[]{:S(2)}, u32[]{:S(2)}) collective-permute-start(bf16[256,1024]{1,0:T(8,128)(2,1)S(1)} %shard_map.74.refs_5_), channel_id=1, source_target_pairs={{0,2},{1,3},{2,4},{3,5},{4,6},{5,7},{6,0},{7,1},{8,10},{9,11},{10,... | collective-permute-start | bytes 1572872 | tf_op jit(solution)/shard_map/ppermute | solution.py:321
  44.6 14.5 %collective-permute-start.15 = (bf16[256,1024]{1,0:T(8,128)(2,1)S(1)}, bf16[256,1024]{1,0:T(8,128)(2,1)S(1)}, u32[]{:S(2)}, u32[]{:S(2)}) collective-permute-start(bf16[256,1024]{1,0:T(8,128)(2,1)S(1)} %shard_map.72.refs_7_), channel_id=1, source_target_pairs={{0,6},{1,7},{2,0},{3,1},{4,2},{5,3},{6,4},{7,5},{8,14},{9,15},{10,... | collective-permute-start | bytes 1572872 | tf_op jit(solution)/shard_map/ppermute | solution.py:321
  47.4 15.9 %collective-permute-start.10 = (bf16[256,512]{1,0:T(8,128)(2,1)S(1)}, bf16[256,512]{1,0:T(8,128)(2,1)S(1)}, u32[]{:S(2)}, u32[]{:S(2)}) collective-permute-start(bf16[256,512]{1,0:T(8,128)(2,1)S(1)} %get-tuple-element.29.refs_5_), channel_id=1, source_target_pairs={{0,2},{1,3},{2,4},{3,5},{4,6},{5,7},{6,0},{7,1},{8,10},{9,11},{10,... | collective-permute-start | bytes 786440 | tf_op jit(solution)/shard_map/ppermute | solution.py:321
  48.8 24.5 %collective-permute-start.9 = (bf16[512,512]{1,0:T(8,128)(2,1)S(1)}, bf16[512,512]{1,0:T(8,128)(2,1)S(1)}, u32[]{:S(2)}, u32[]{:S(2)}) collective-permute-start(bf16[512,512]{1,0:T(8,128)(2,1)S(1)} %get-tuple-element.31), channel_id=1, source_target_pairs={{0,1},{1,0},{2,3},{3,2},{4,5},{5,4},{6,7},{7,6},{8,9},{9,8},{10,11... | collective-permute-start | bytes 1572872 | tf_op jit(solution)/shard_map/ppermute | solution.py:321
  50.0 19.5 %collective-permute-start.11 = (bf16[256,512]{1,0:T(8,128)(2,1)S(1)}, bf16[256,512]{1,0:T(8,128)(2,1)S(1)}, u32[]{:S(2)}, u32[]{:S(2)}) collective-permute-start(bf16[256,512]{1,0:T(8,128)(2,1)S(1)} %get-tuple-element.32), channel_id=1, source_target_pairs={{0,3},{1,2},{2,5},{3,4},{4,7},{5,6},{6,1},{7,0},{8,11},{9,10},{10,... | collective-permute-start | bytes 786440 | tf_op jit(solution)/shard_map/ppermute | solution.py:321
  57.7 12.9 %collective-permute-start.12 = (bf16[256,512]{1,0:T(8,128)(2,1)S(1)}, bf16[256,512]{1,0:T(8,128)(2,1)S(1)}, u32[]{:S(2)}, u32[]{:S(2)}) collective-permute-start(bf16[256,512]{1,0:T(8,128)(2,1)S(1)} %get-tuple-element.33), channel_id=1, source_target_pairs={{0,6},{1,7},{2,0},{3,1},{4,2},{5,3},{6,4},{7,5},{8,14},{9,15},{10,... | collective-permute-start | bytes 786440 | tf_op jit(solution)/shard_map/ppermute | solution.py:321
  59.1 14.2 %collective-permute-start.13 = (bf16[256,512]{1,0:T(8,128)(2,1)S(1)}, bf16[256,512]{1,0:T(8,128)(2,1)S(1)}, u32[]{:S(2)}, u32[]{:S(2)}) collective-permute-start(bf16[256,512]{1,0:T(8,128)(2,1)S(1)} %get-tuple-element.34), channel_id=1, source_target_pairs={{0,7},{1,6},{2,1},{3,0},{4,3},{5,2},{6,5},{7,4},{8,15},{9,14},{10,... | collective-permute-start | bytes 786440 | tf_op jit(solution)/shard_map/ppermute | solution.py:321
  63.3 12.0 %collective-permute-start.16 = (bf16[256,512]{1,0:T(8,128)(2,1)S(1)}, bf16[256,512]{1,0:T(8,128)(2,1)S(1)}, u32[]{:S(2)}, u32[]{:S(2)}) collective-permute-start(bf16[256,512]{1,0:T(8,128)(2,1)S(1)} %get-tuple-element.35), channel_id=1, source_target_pairs={{0,6},{1,7},{2,0},{3,1},{4,2},{5,3},{6,4},{7,5},{8,14},{9,15},{10,... | collective-permute-start | bytes 786440 | tf_op jit(solution)/shard_map/ppermute | solution.py:321
  69.4 13.4 %collective-permute-start.17 = (bf16[256,512]{1,0:T(8,128)(2,1)S(1)}, bf16[256,512]{1,0:T(8,128)(2,1)S(1)}, u32[]{:S(2)}, u32[]{:S(2)}) collective-permute-start(bf16[256,512]{1,0:T(8,128)(2,1)S(1)} %get-tuple-element.36), channel_id=1, source_target_pairs={{0,7},{1,6},{2,1},{3,0},{4,3},{5,2},{6,5},{7,4},{8,15},{9,14},{10,... | collective-permute-start | bytes 786440 | tf_op jit(solution)/shard_map/ppermute | solution.py:321
  70.6 12.3 %collective-permute-start.18 = (bf16[256,512]{1,0:T(8,128)(2,1)S(1)}, bf16[256,512]{1,0:T(8,128)(2,1)S(1)}, u32[]{:S(2)}, u32[]{:S(2)}) collective-permute-start(bf16[256,512]{1,0:T(8,128)(2,1)S(1)} %get-tuple-element.37), channel_id=1, source_target_pairs={{0,2},{1,3},{2,4},{3,5},{4,6},{5,7},{6,0},{7,1},{8,10},{9,11},{10,... | collective-permute-start | bytes 786440 | tf_op jit(solution)/shard_map/ppermute | solution.py:321
  73.2 12.2 %collective-permute-start.19 = (bf16[256,512]{1,0:T(8,128)(2,1)S(1)}, bf16[256,512]{1,0:T(8,128)(2,1)S(1)}, u32[]{:S(2)}, u32[]{:S(2)}) collective-permute-start(bf16[256,512]{1,0:T(8,128)(2,1)S(1)} %get-tuple-element.38), channel_id=1, source_target_pairs={{0,3},{1,2},{2,5},{3,4},{4,7},{5,6},{6,1},{7,0},{8,11},{9,10},{10,... | collective-permute-start | bytes 786440 | tf_op jit(solution)/shard_map/ppermute | solution.py:321

commit v2 on v1

--- a/solution.py
+++ b/solution.py
@@ -170,12 +170,22 @@
     )
 
 
-def local_attention(q, k, v):
+def local_attention(q, k, v, bring, after):
     count, width = q.shape
     heads = width // HEAD_DIM
     blocks = count // BLOCK
 
-    def kernel(q_ref, k_ref, v_ref, w_ref, e_ref):
+    deep, wide = bring[0].shape
+    n_b = len(bring)
+
+    def kernel(q_ref, k_ref, v_ref, *refs):
+        b_hbm, (w_ref, e_ref, b_ref, sem) = refs[:n_b], refs[n_b + 1 :]
+        moves = [
+            pltpu.make_async_copy(source, b_ref.at[pl.ds(i * deep, deep), :], sem.at[i])
+            for i, source in enumerate(b_hbm)
+        ]
+        for move in moves:
+            move.start()
         rows = lax.broadcasted_iota(jnp.int32, (BLOCK, BLOCK), 0)
         cols = lax.broadcasted_iota(jnp.int32, (BLOCK, BLOCK), 1)
         keep = rows >= cols
@@ -190,19 +200,26 @@
                 e_ref[b, at_h, :] = state
                 if b < blocks - 1:
                     state = state + dot_t(kb, vb, 0, 0)
-
-    return call(
-        kernel,
-        [IN_VMEM] * 3,
-        [pltpu.VMEM((count, width), F32), pltpu.VMEM((blocks, width, HEAD_DIM), F32)],
-        (q, k, v),
+        for move in moves:
+            move.wait()
+
+    return call(
+        kernel,
+        [IN_VMEM] * 3 + [IN_HBM] * n_b + [pl.BlockSpec(memory_space=pl.ANY)],
+        [
+            pltpu.VMEM((count, width), F32),
+            pltpu.VMEM((blocks, width, HEAD_DIM), F32),
+            pltpu.VMEM((n_b * deep, wide), BF16),
+        ],
+        (q, k, v, *map(streamed, bring), after),
         4 * count * width * (BLOCK + HEAD_DIM),
-        14 * count * width,
-        8,
-    )
-
-
-def attend(place, index, q, within, earlier, from_x, from_z, gain, mine, block, after=()):
+        14 * count * width + 2 * n_b * deep * wide,
+        12,
+        [pltpu.SemaphoreType.DMA((n_b,))],
+    )
+
+
+def attend(place, index, q, within, earlier, from_x, from_z, gain, mine):
     count, width = q.shape
     heads = width // HEAD_DIM
     per_half = count // BLOCK // 2
@@ -212,101 +229,80 @@
         xs, zs, g_ref, o_ref = refs[:hops], refs[hops : 2 * hops], refs[2 * hops], refs[-1]
         half = place_ref[0] % 2 if mine else 1 - place_ref[0] % 2
         at_x, at_z = index_ref[0] % RING, index_ref[0] // RING
-        here = half * per_half + block
-        rows = pl.ds(pl.multiple_of(here * BLOCK, BLOCK), BLOCK)
         for h in range(heads):
             cols = slice(h * HEAD_DIM, (h + 1) * HEAD_DIM)
-            state = e_ref[here, cols, :]
+            carried = jnp.zeros((HEAD_DIM, HEAD_DIM), F32)
             for at, came in ((at_x, xs), (at_z, zs)):
                 for shift, ref in zip(SHIFTS, came):
                     source = (at - shift + RING) % RING
-                    state += jnp.where(source < at, ref[cols, :].astype(F32), 0.0)
-            raw = w_ref[rows, cols] + dot(q_ref[rows, cols], state.astype(BF16))
-            power = jnp.mean(raw * raw, axis=-1, keepdims=True)
-            o_ref[:, cols] = (raw * lax.rsqrt(power + 1e-06) * g_ref[:, cols]).astype(BF16)
-
-    return call(
-        kernel,
-        [IN_SMEM] * 2
-        + [IN_VMEM] * (4 + 2 * hops)
-        + [pl.BlockSpec(memory_space=pl.ANY)] * len(after),
-        pltpu.VMEM((BLOCK, width), BF16),
-        (place, index, q, within, earlier, *from_x, *from_z, gain, *after),
-        count * width * HEAD_DIM // 2,
-        2 * count * width,
+                    carried += jnp.where(source < at, ref[cols, :].astype(F32), 0.0)
+            for b in range(per_half):
+                here = half * per_half + b
+                rows = pl.ds(pl.multiple_of(here * BLOCK, BLOCK), BLOCK)
+                prior = (carried + e_ref[here, cols, :]).astype(BF16)
+                raw = w_ref[rows, cols] + dot(q_ref[rows, cols], prior)
+                power = jnp.mean(raw * raw, axis=-1, keepdims=True)
+                o_ref[b * BLOCK : (b + 1) * BLOCK, cols] = (
+                    raw * lax.rsqrt(power + 1e-06) * g_ref[:, cols]
+                ).astype(BF16)
+
+    return call(
+        kernel,
+        [IN_SMEM] * 2 + [IN_VMEM] * (4 + 2 * hops),
+        pltpu.VMEM((count // 2, width), BF16),
+        (place, index, q, within, earlier, *from_x, *from_z, gain),
+        count * width * HEAD_DIM,
+        4 * count * width,
         8,
     )
 
 
-def out_project(place, mine, theirs, w_out, pieces, form, added=(), after=()):
-    size, width = mine[0].shape
-    n_p = len(pieces)
+STRAIGHT, CROSS = 0, 1
+
+
+def out_project(place, mine, theirs, w_out, blocks, added=()):
+    rows, width = mine.shape
+
+    def kernel(place_ref, x_ref, y_ref, w_ref, *refs):
+        adds, outs = refs[: len(added)], refs[len(added) :]
+        y, c = place_ref[0] // 2, place_ref[0] % 2
+        for p, (step, side) in enumerate(blocks):
+            owner = ((y + step + RING) % RING) * 2 + (c if side == STRAIGHT else 1 - c)
+            cols = pl.ds(pl.multiple_of(owner * width, width), width)
+            total = dot(x_ref[...], w_ref[:width, cols]) + dot(y_ref[...], w_ref[width:, cols])
+            if added:
+                total = total + adds[p][...].astype(F32)
+            outs[p][...] = total.astype(BF16)
+
+    return call(
+        kernel,
+        [IN_SMEM] + [IN_VMEM] * (3 + len(added)),
+        [pltpu.VMEM((rows, width), BF16)] * len(blocks),
+        (place, mine, theirs, w_out, *added),
+        4 * len(blocks) * rows * width * width,
+        4 * len(blocks) * width * width,
+        12,
+    )
+
+
+def final_sum(place, own, near, late):
+    rows, width = own[0].shape
 
     def kernel(place_ref, *refs):
-        xs, ys, w_ref = refs[:2], refs[2:4], refs[4]
-        adds, outs = refs[5 : 5 + len(added)], refs[5 + len(added) + len(after) :]
-        y, c = place_ref[0] // 2, place_ref[0] % 2
-        for p, (block, step) in enumerate(pieces):
-            chip = (y + step + RING) % RING
-            for side in range(2):
-                core = c if side == 0 else 1 - c
-                cols = pl.ds(pl.multiple_of((chip * 2 + core) * width, width), width)
-                total = dot(xs[block][...], w_ref[:width, cols])
-                total = total + dot(ys[block][...], w_ref[width:, cols])
-                here = slice(side * width, (side + 1) * width)
-                if added:
-                    total = total + adds[p][:, here].astype(F32)
-                total = total.astype(BF16)
-                if form == "joined":
-                    outs[p][:, here] = total
-                elif form == "apart":
-                    outs[2 * p + side][...] = total
-                else:
-                    outs[side][p * size : (p + 1) * size, :] = total
-
-    if form == "joined":
-        out_shape = [pltpu.VMEM((size, 2 * width), BF16)] * n_p
-    elif form == "apart":
-        out_shape = [pltpu.VMEM((size, width), BF16)] * (2 * n_p)
-    else:
-        out_shape = [pltpu.VMEM((n_p * size, width), BF16)] * 2
-    return call(
-        kernel,
-        [IN_SMEM]
-        + [IN_VMEM] * (5 + len(added))
-        + [pl.BlockSpec(memory_space=pl.ANY)] * len(after),
-        out_shape,
-        (place, *mine, *theirs, w_out, *added, *after),
-        8 * n_p * size * width * width,
-        8 * width * width,
-        12,
-    )
-
-
-def final_sum(place, own, own_cross, near, late, count):
-    size, width = near[0][0].shape
-
-    def kernel(place_ref, own_ref, cross_ref, *refs):
         o_ref = refs[-1]
         c = place_ref[0] % 2
-        for which, base in enumerate((own_ref, cross_ref)):
-            half = c if which == 0 else 1 - c
-            for b in range(2):
-                at = slice(b * size, (b + 1) * size)
-                total = base[at, :].astype(F32)
-                total = total + refs[2 * b + which][...].astype(F32)
-                total = total + refs[4 + 2 * b + which][...].astype(F32)
-                start = pl.multiple_of(half * (2 * size) + b * size, size)
-                o_ref[pl.ds(start, size), :] = total.astype(BF16)
-
-    terms = [a for pair in near for a in pair] + [a for pair in late for a in pair]
-    return call(
-        kernel,
-        [IN_SMEM] + [IN_VMEM] * (2 + len(terms)),
-        jax.ShapeDtypeStruct((count, width), BF16),
-        (place, own, own_cross, *terms),
-        12 * size * width,
-        24 * size * width,
+        for which in range(2):
+            terms = [refs[2 * i + which][...].astype(F32) for i in range(3)]
+            start = pl.multiple_of((c if which == 0 else 1 - c) * rows, rows)
+            o_ref[pl.ds(start, rows), :] = (terms[0] + terms[1] + terms[2]).astype(BF16)
+
+    return call(
+        kernel,
+        [IN_SMEM] + [IN_VMEM] * 6,
+        jax.ShapeDtypeStruct((2 * rows, width), BF16),
+        (place, *own, *near, *late),
+        6 * rows * width,
+        16 * rows * width,
         8,
     )
 
@@ -334,48 +330,36 @@
     index = lax.axis_index("seq").astype(jnp.int32).reshape(1)
 
     w_theirs = lax.ppermute(w_out, "head", [(h, h ^ 1) for h in range(2 * RING)])
-    keys, values, total = project(tokens, [w_key, w_value], slice(0, count), states=True)
+    keys, values, total = project(
+        tokens, [w_key, w_value], slice(0, count), states=True, after=(place, index)
+    )
     from_x = [seq_send(total, 0, d) for d in SHIFTS]
-    cut = count - BLOCK
-    queries, w_held = project(
-        tokens, [w_query], slice(0, cut), after=(total,), bring=(w_out, w_theirs)
-    )
+    (queries,) = project(tokens, [w_query], slice(0, count), after=(total,))
     row = row_total(total, from_x, queries)
     from_z = [seq_send(row, d, 0) for d in SHIFTS]
-    (queries,) = project(tokens, [w_query], slice(cut, count), after=(row,), into=queries)
-    within, earlier = local_attention(queries, keys, values)
-
-    def attended(mine, block, **kw):
+    within, earlier, w_held = local_attention(
+        queries, keys, values, (w_out, w_theirs), row
+    )
+
+    def attended(mine):
         gain = norm_gain.reshape(1, -1)
-        return attend(
-            place, index, queries, within, earlier, from_x, from_z, gain, mine, block, **kw
-        )
-
-    def project_out(pieces, form, blocks=(0, 1), **kw):
-        x, y = [mine[b] for b in blocks], [theirs[b] for b in blocks]
-        return out_project(place, x, y, w_held, pieces, form, **kw)
-
-    other0 = attended(False, 0)
-    other1 = attended(False, 1, after=(other0,))
-    theirs = [head_send(other0, 0, 1), head_send(other1, 0, 1)]
-    mine = [attended(True, 0, after=(other1,))]
-    (far0,) = project_out([(0, 2)], "joined", blocks=(0, 0))
-    mine.append(attended(True, 1, after=(far0,)))
-    (far1,) = project_out([(0, 2)], "joined", blocks=(1, 1))
-    near = project_out([(0, 1), (1, -1)], "apart", after=(far1,))
-    far0, far1 = head_send(far0, -1), head_send(far1, 1)
-
-    def last_hop(up_s, up_x, down_s, down_x):
-        up, down = head_send(up_s, 1), head_send(down_s, -1)
-        up_x = head_send(up_x, 1, 1)
-        return (up, up_x), (down, head_send(down_x, -1, 1))
-
-    own, own_cross = project_out([(0, 0), (1, 0)], "stacked", after=(near[0],))
-    near = last_hop(*near)
-    own_cross = head_send(own_cross, 0, 1)
-    late = project_out([(1, 1), (0, -1)], "apart", added=(far1, far0))
-    late = last_hop(*late)[::-1]
-    return final_sum(place, own, own_cross, near, late, count)
+        return attend(place, index, queries, within, earlier, from_x, from_z, gain, mine)
+
+    theirs = head_send(attended(False), 0, 1)
+    mine = attended(True)
+
+    def project_out(blocks, **kw):
+        return out_project(place, mine, theirs, w_held, blocks, **kw)
+
+    far_s, far_x = project_out([(2, STRAIGHT), (2, CROSS)])
+    far_s, far_x = head_send(far_s, -1), head_send(far_x, 1)
+    near_s, near_x = project_out([(1, STRAIGHT), (-1, CROSS)])
+    near = head_send(near_s, 1), head_send(near_x, -1, 1)
+    own_s, own_x = project_out([(0, STRAIGHT), (0, CROSS)])
+    own = own_s, head_send(own_x, 0, 1)
+    late_s, late_x = project_out([(-1, STRAIGHT), (1, CROSS)], added=(far_s, far_x))
+    late = head_send(late_s, -1), head_send(late_x, 1, 1)
+    return final_sum(place, own, near, late)
 
 
 def solution(mesh):

time: 87 us -> 82.2 us (0.945)
  Pallas kernels: 35.3 us -> 30.1 us
  waiting for transfers between devices: 26.2 us -> 28.8 us
  starting transfers between devices: 25.1 us -> 23.1 us
    pallas_call x15 -> x11, Pallas kernels: 35.3 us -> 30.1 us  [call(): pl.pallas_call(kernel, in_specs=in_specs, out_specs=jax.tree.map(lambda _...]
    ppermute x6, waiting for transfers between devices: 0.02 us -> 2.27 us  [seq_send(): return held(lax.ppermute(x, 'seq', pairs))]
    ppermute x13 -> x8, starting transfers between devices: 14.1 us -> 12.2 us  [head_send(): return held(lax.ppermute(x, 'head', pairs))]
    ppermute x13 -> x8, waiting for transfers between devices: 26.2 us -> 26.5 us  [head_send(): return held(lax.ppermute(x, 'head', pairs))]
  transfers between devices with their start and end apart: 20 -> 15, of which waited for: 8 -> 8; matrix products, arithmetic and copies ran while one was open for 0% -> 0% of each run, Pallas kernels for 38% -> 33%
where the time goes in v2:
time: 82.2 us; the launch traced here: 82.1 us
  Pallas kernels  30.1 us (37%)
  waiting for transfers between devices  28.8 us (35%)
  starting transfers between devices  23.1 us (28%)
    pallas_call x11, Pallas kernels, call(): pl.pallas_call(kernel, in_specs=in_specs, out_specs=jax.tree.map(lambda _...  30.1 us
    ppermute x8, waiting for transfers between devices, head_send(): return held(lax.ppermute(x, 'head', pairs))  26.5 us
    ppermute x8, starting transfers between devices, head_send(): return held(lax.ppermute(x, 'head', pairs))  12.2 us
    ppermute x6, starting transfers between devices, seq_send(): return held(lax.ppermute(x, 'seq', pairs))  9.53 us
    ppermute x6, waiting for transfers between devices, seq_send(): return held(lax.ppermute(x, 'seq', pairs))  2.27 us
  transfers between devices with their start and end apart: 15, of which 8 were waited for; matrix products, arithmetic and copies ran while one was open for 0% of the time, Pallas kernels for 33%

profile of v2, /device:TPU:1, one launch (start us, length us, event | category | flops | bytes accessed | tf_op | source)
XLA Modules:
  0.0 82.1 jit_solution(18208360213498389115)
XLA Ops:
  0.0 1.4 %collective-permute-start = (bf16[512,4096]{1,0:T(8,128)(2,1)}, bf16[512,4096]{1,0:T(8,128)(2,1)}, u32[]{:S(2)}, u32[]{:S(2)}) collective-permute-start(bf16[512,4096]{1,0:T(8,128)(2,1)} %refs_0_.5), channel_id=1, source_target_pairs={{0,1},{1,0},{2,3},{3,2},{4,5},{5,4},{6,7},{7,6},{8,9},{9,8},{10,11... | collective-permute-start | bytes 12582920 | tf_op jit(solution)/shard_map/ppermute | solution.py:332
  1.4 12.0 %shard_map.64 = (bf16[1024,512]{1,0:T(8,128)(2,1)S(1)}, bf16[1024,512]{1,0:T(8,128)(2,1)S(1)}, bf16[512,128]{1,0:T(8,128)(2,1)S(1)}) custom-call(bf16[1024,4096]{1,0:T(8,128)(2,1)} %refs_0_.4, bf16[4096,512]{1,0:T(8,128)(2,1)} %refs_1_.2, bf16[4096,512]{1,0:T(8,128)(2,1)} %refs_2_.1, s32[1]{0:T(128)} %bitcast.refs_3_.place_ref, s32[1]{0:T(128)} %bitcast.1.refs_4_.index_ref), custom_call_target="tpu_custom_call" | custom-call | flops 8589934592 | bytes 16777216 | tf_op jit(solution)/shard_map/pallas_call | solution.py:27
  13.4 1.4 %collective-permute-start.1 = (bf16[512,128]{1,0:T(8,128)(2,1)S(1)}, bf16[512,128]{1,0:T(8,128)(2,1)S(1)}, u32[]{:S(2)}, u32[]{:S(2)}) collective-permute-start(bf16[512,128]{1,0:T(8,128)(2,1)S(1)} %get-tuple-element.19.refs_2_.refs_0_), channel_id=1, source_target_pairs={{0,8},{8,16},{16,24},{24,0},{32,40},{40,48},{48,56},{56,32},{64,72... | collective-permute-start | bytes 393224 | tf_op jit(solution)/shard_map/ppermute | solution.py:324
  14.8 1.3 %collective-permute-start.2 = (bf16[512,128]{1,0:T(8,128)(2,1)S(1)}, bf16[512,128]{1,0:T(8,128)(2,1)S(1)}, u32[]{:S(2)}, u32[]{:S(2)}) collective-permute-start(bf16[512,128]{1,0:T(8,128)(2,1)S(1)} %get-tuple-element.19.refs_2_.refs_0_), channel_id=1, source_target_pairs={{0,24},{8,0},{16,8},{24,16},{32,56},{40,32},{48,40},{56,48},{64,88... | collective-permute-start | bytes 393224 | tf_op jit(solution)/shard_map/ppermute | solution.py:324
  16.2 1.6 %collective-permute-start.3 = (bf16[512,128]{1,0:T(8,128)(2,1)S(1)}, bf16[512,128]{1,0:T(8,128)(2,1)S(1)}, u32[]{:S(2)}, u32[]{:S(2)}) collective-permute-start(bf16[512,128]{1,0:T(8,128)(2,1)S(1)} %get-tuple-element.19.refs_2_.refs_0_), channel_id=1, source_target_pairs={{0,16},{8,24},{16,0},{24,8},{32,48},{40,56},{48,32},{56,40},{64,80... | collective-permute-start | bytes 393224 | tf_op jit(solution)/shard_map/ppermute | solution.py:324
  17.8 7.0 %shard_map.65.refs_4_.q_ref = bf16[1024,512]{1,0:T(8,128)(2,1)S(1)} custom-call(bf16[1024,4096]{1,0:T(8,128)(2,1)} %refs_0_.4, bf16[4096,512]{1,0:T(8,128)(2,1)} %refs_1_.3, bf16[512,128]{1,0:T(8,128)(2,1)S(1)} %get-tuple-element.19.refs_2_.refs_0_), custom_call_target="tpu_custom_call" | custom-call | flops 4294967296 | bytes 12582912 | tf_op jit(solution)/shard_map/pallas_call | solution.py:27
  24.9 1.7 %collective-permute-start.4 = (bf16[512,128]{1,0:T(8,128)(2,1)S(1)}, bf16[512,128]{1,0:T(8,128)(2,1)S(1)}, u32[]{:S(2)}, u32[]{:S(2)}) collective-permute-start(bf16[512,128]{1,0:T(8,128)(2,1)S(1)} %shard_map.66.refs_2_), channel_id=1, source_target_pairs={{0,32},{8,40},{16,48},{24,56},{32,64},{40,72},{48,80},{56,88},{64,... | collective-permute-start | bytes 393224 | tf_op jit(solution)/shard_map/ppermute | solution.py:324
  26.6 2.2 %collective-permute-start.5 = (bf16[512,128]{1,0:T(8,128)(2,1)S(1)}, bf16[512,128]{1,0:T(8,128)(2,1)S(1)}, u32[]{:S(2)}, u32[]{:S(2)}) collective-permute-start(bf16[512,128]{1,0:T(8,128)(2,1)S(1)} %shard_map.66.refs_2_), channel_id=1, source_target_pairs={{0,96},{8,104},{16,112},{24,120},{32,0},{40,8},{48,16},{56,24},{64... | collective-permute-start | bytes 393224 | tf_op jit(solution)/shard_map/ppermute | solution.py:324
  30.1 3.5 %shard_map.67 = (f32[1024,512]{1,0:T(8,128)S(1)}, f32[4,512,128]{2,1,0:T(8,128)S(1)}, bf16[1024,4096]{1,0:T(8,128)(2,1)S(1)}) custom-call(bf16[1024,512]{1,0:T(8,128)(2,1)S(1)} %shard_map.65.refs_4_.q_ref, bf16[1024,512]{1,0:T(8,128)(2,1)S(1)} %get-tuple-element.20.k_ref, bf16[1024,512]{1,0:T(8,128)(2,1)S(1)} %get-tuple-element.21.v_ref, ...), custom_call_target="tpu_custom_call" | custom-call | flops 805306368 | bytes 15728640 | tf_op jit(solution)/shard_map/pallas_call | solution.py:27
  33.6 2.3 %collective-permute-done.6.refs_5_ = bf16[512,128]{1,0:T(8,128)(2,1)S(1)} collective-permute-done((bf16[512,128]{1,0:T(8,128)(2,1)S(1)}, bf16[512,128]{1,0:T(8,128)(2,1)S(1)}, u32[]{:S(2)}, u32[]{:S(2)}) %collective-permute-start.6) | collective-permute-done | bytes 131104 | tf_op jit(solution)/shard_map/ppermute | solution.py:324
  36.4 1.4 %collective-permute-start.7 = (bf16[512,512]{1,0:T(8,128)(2,1)S(1)}, bf16[512,512]{1,0:T(8,128)(2,1)S(1)}, u32[]{:S(2)}, u32[]{:S(2)}) collective-permute-start(bf16[512,512]{1,0:T(8,128)(2,1)S(1)} %shard_map.69), channel_id=1, source_target_pairs={{0,1},{1,0},{2,3},{3,2},{4,5},{5,4},{6,7},{7,6},{8,9},{9,8},{10,11... | collective-permute-start | bytes 1572872 | tf_op jit(solution)/shard_map/ppermute | solution.py:317
  40.7 2.8 %collective-permute-start.11 = (bf16[512,512]{1,0:T(8,128)(2,1)S(1)}, bf16[512,512]{1,0:T(8,128)(2,1)S(1)}, u32[]{:S(2)}, u32[]{:S(2)}) collective-permute-start(bf16[512,512]{1,0:T(8,128)(2,1)S(1)} %get-tuple-element.29), channel_id=1, source_target_pairs={{0,6},{1,7},{2,0},{3,1},{4,2},{5,3},{6,4},{7,5},{8,14},{9,15},{10,... | collective-permute-start | bytes 1572872 | tf_op jit(solution)/shard_map/ppermute | solution.py:317
  43.5 1.2 %shard_map.71 = (bf16[512,512]{1,0:T(8,128)(2,1)S(1)}, bf16[512,512]{1,0:T(8,128)(2,1)S(1)}) custom-call(s32[1]{0:T(128)} %bitcast.refs_3_.place_ref, bf16[512,512]{1,0:T(8,128)(2,1)S(1)} %shard_map.68.x_ref, bf16[512,512]{1,0:T(8,128)(2,1)S(1)} %collective-permute-done.7.y_ref, bf16[1024,4096]{1,0:T(8,128)(2,1)S(1)} %get-tuple-element.24.w_ref), custom_call_target="tpu_custom_call" | custom-call | flops 1073741824 | bytes 2097152 | tf_op jit(solution)/shard_map/pallas_call | solution.py:27
  44.7 3.6 %collective-permute-start.10 = (bf16[512,512]{1,0:T(8,128)(2,1)S(1)}, bf16[512,512]{1,0:T(8,128)(2,1)S(1)}, u32[]{:S(2)}, u32[]{:S(2)}) collective-permute-start(bf16[512,512]{1,0:T(8,128)(2,1)S(1)} %get-tuple-element.28), channel_id=1, source_target_pairs={{0,7},{1,6},{2,1},{3,0},{4,3},{5,2},{6,5},{7,4},{8,15},{9,14},{10,... | collective-permute-start | bytes 1572872 | tf_op jit(solution)/shard_map/ppermute | solution.py:317
  48.3 1.2 %shard_map.70 = (bf16[512,512]{1,0:T(8,128)(2,1)S(1)}, bf16[512,512]{1,0:T(8,128)(2,1)S(1)}) custom-call(s32[1]{0:T(128)} %bitcast.refs_3_.place_ref, bf16[512,512]{1,0:T(8,128)(2,1)S(1)} %shard_map.68.x_ref, bf16[512,512]{1,0:T(8,128)(2,1)S(1)} %collective-permute-done.7.y_ref, bf16[1024,4096]{1,0:T(8,128)(2,1)S(1)} %get-tuple-element.24.w_ref), custom_call_target="tpu_custom_call" | custom-call | flops 1073741824 | bytes 2097152 | tf_op jit(solution)/shard_map/pallas_call | solution.py:27
  49.6 4.7 %collective-permute-done.11.refs_0_ = bf16[512,512]{1,0:T(8,128)(2,1)S(1)} collective-permute-done((bf16[512,512]{1,0:T(8,128)(2,1)S(1)}, bf16[512,512]{1,0:T(8,128)(2,1)S(1)}, u32[]{:S(2)}, u32[]{:S(2)}) %collective-permute-start.11) | collective-permute-done | bytes 524320 | tf_op jit(solution)/shard_map/ppermute | solution.py:317
  54.4 3.1 %collective-permute-done.12.refs_1_ = bf16[512,512]{1,0:T(8,128)(2,1)S(1)} collective-permute-done((bf16[512,512]{1,0:T(8,128)(2,1)S(1)}, bf16[512,512]{1,0:T(8,128)(2,1)S(1)}, u32[]{:S(2)}, u32[]{:S(2)}) %collective-permute-start.12) | collective-permute-done | bytes 524320 | tf_op jit(solution)/shard_map/ppermute | solution.py:317
  57.5 1.3 %shard_map.73 = (bf16[512,512]{1,0:T(8,128)(2,1)S(1)}, bf16[512,512]{1,0:T(8,128)(2,1)S(1)}) custom-call(s32[1]{0:T(128)} %bitcast.refs_3_.place_ref, bf16[512,512]{1,0:T(8,128)(2,1)S(1)} %shard_map.68.x_ref, bf16[512,512]{1,0:T(8,128)(2,1)S(1)} %collective-permute-done.7.y_ref, bf16[1024,4096]{1,0:T(8,128)(2,1)S(1)} %get-tuple-element.24.w_ref, ...), custom_call_target="tpu_custom_call" | custom-call | flops 1073741824 | bytes 2097152 | tf_op jit(solution)/shard_map/pallas_call | solution.py:27
  59.1 4.0 %collective-permute-start.14 = (bf16[512,512]{1,0:T(8,128)(2,1)S(1)}, bf16[512,512]{1,0:T(8,128)(2,1)S(1)}, u32[]{:S(2)}, u32[]{:S(2)}) collective-permute-start(bf16[512,512]{1,0:T(8,128)(2,1)S(1)} %get-tuple-element.32), channel_id=1, source_target_pairs={{0,3},{1,2},{2,5},{3,4},{4,7},{5,6},{6,1},{7,0},{8,11},{9,10},{10,... | collective-permute-start | bytes 1572872 | tf_op jit(solution)/shard_map/ppermute | solution.py:317
  63.1 3.7 %collective-permute-done.10.refs_3_ = bf16[512,512]{1,0:T(8,128)(2,1)S(1)} collective-permute-done((bf16[512,512]{1,0:T(8,128)(2,1)S(1)}, bf16[512,512]{1,0:T(8,128)(2,1)S(1)}, u32[]{:S(2)}, u32[]{:S(2)}) %collective-permute-start.10) | collective-permute-done | bytes 524320 | tf_op jit(solution)/shard_map/ppermute | solution.py:317
  66.7 2.0 %collective-permute-done.9.refs_2_ = bf16[512,512]{1,0:T(8,128)(2,1)S(1)} collective-permute-done((bf16[512,512]{1,0:T(8,128)(2,1)S(1)}, bf16[512,512]{1,0:T(8,128)(2,1)S(1)}, u32[]{:S(2)}, u32[]{:S(2)}) %collective-permute-start.9) | collective-permute-done | bytes 524320 | tf_op jit(solution)/shard_map/ppermute | solution.py:317
  68.7 8.1 %collective-permute-done.13.refs_4_ = bf16[512,512]{1,0:T(8,128)(2,1)S(1)} collective-permute-done((bf16[512,512]{1,0:T(8,128)(2,1)S(1)}, bf16[512,512]{1,0:T(8,128)(2,1)S(1)}, u32[]{:S(2)}, u32[]{:S(2)}) %collective-permute-start.13) | collective-permute-done | bytes 524320 | tf_op jit(solution)/shard_map/ppermute | solution.py:317
  76.8 4.0 %collective-permute-done.14.refs_5_ = bf16[512,512]{1,0:T(8,128)(2,1)S(1)} collective-permute-done((bf16[512,512]{1,0:T(8,128)(2,1)S(1)}, bf16[512,512]{1,0:T(8,128)(2,1)S(1)}, u32[]{:S(2)}, u32[]{:S(2)}) %collective-permute-start.14) | collective-permute-done | bytes 524320 | tf_op jit(solution)/shard_map/ppermute | solution.py:317
  80.8 1.3 %shard_map.74 = bf16[1024,512]{1,0:T(8,128)(2,1)} custom-call(s32[1]{0:T(128)} %bitcast.refs_3_.place_ref, bf16[512,512]{1,0:T(8,128)(2,1)S(1)} %get-tuple-element.25.refs_0_, bf16[512,512]{1,0:T(8,128)(2,1)S(1)} %collective-permute-done.8.refs_1_, bf16[512,512]{1,0:T(8,128)(2,1)S(1)} %collective-permute-done.9.refs_2_, ...), custom_call_target="tpu_custom_call" | custom-call | flops 1572864 | bytes 4194304 | tf_op jit(solution)/shard_map/pallas_call | solution.py:27
  (19 shorter events, 5.1 us)
Async XLA Ops:
  0.0 30.0 %collective-permute-start = (bf16[512,4096]{1,0:T(8,128)(2,1)}, bf16[512,4096]{1,0:T(8,128)(2,1)}, u32[]{:S(2)}, u32[]{:S(2)}) collective-permute-start(bf16[512,4096]{1,0:T(8,128)(2,1)} %refs_0_.5), channel_id=1, source_target_pairs={{0,1},{1,0},{2,3},{3,2},{4,5},{5,4},{6,7},{7,6},{8,9},{9,8},{10,11... | collective-permute-start | bytes 12582920 | tf_op jit(solution)/shard_map/ppermute | solution.py:332
  13.4 11.4 %collective-permute-start.1 = (bf16[512,128]{1,0:T(8,128)(2,1)S(1)}, bf16[512,128]{1,0:T(8,128)(2,1)S(1)}, u32[]{:S(2)}, u32[]{:S(2)}) collective-permute-start(bf16[512,128]{1,0:T(8,128)(2,1)S(1)} %get-tuple-element.19.refs_2_.refs_0_), channel_id=1, source_target_pairs={{0,8},{8,16},{16,24},{24,0},{32,40},{40,48},{48,56},{56,32},{64,72... | collective-permute-start | bytes 393224 | tf_op jit(solution)/shard_map/ppermute | solution.py:324
  14.8 10.0 %collective-permute-start.2 = (bf16[512,128]{1,0:T(8,128)(2,1)S(1)}, bf16[512,128]{1,0:T(8,128)(2,1)S(1)}, u32[]{:S(2)}, u32[]{:S(2)}) collective-permute-start(bf16[512,128]{1,0:T(8,128)(2,1)S(1)} %get-tuple-element.19.refs_2_.refs_0_), channel_id=1, source_target_pairs={{0,24},{8,0},{16,8},{24,16},{32,56},{40,32},{48,40},{56,48},{64,88... | collective-permute-start | bytes 393224 | tf_op jit(solution)/shard_map/ppermute | solution.py:324
  16.2 8.7 %collective-permute-start.3 = (bf16[512,128]{1,0:T(8,128)(2,1)S(1)}, bf16[512,128]{1,0:T(8,128)(2,1)S(1)}, u32[]{:S(2)}, u32[]{:S(2)}) collective-permute-start(bf16[512,128]{1,0:T(8,128)(2,1)S(1)} %get-tuple-element.19.refs_2_.refs_0_), channel_id=1, source_target_pairs={{0,16},{8,24},{16,0},{24,8},{32,48},{40,56},{48,32},{56,40},{64,80... | collective-permute-start | bytes 393224 | tf_op jit(solution)/shard_map/ppermute | solution.py:324
  24.9 8.6 %collective-permute-start.4 = (bf16[512,128]{1,0:T(8,128)(2,1)S(1)}, bf16[512,128]{1,0:T(8,128)(2,1)S(1)}, u32[]{:S(2)}, u32[]{:S(2)}) collective-permute-start(bf16[512,128]{1,0:T(8,128)(2,1)S(1)} %shard_map.66.refs_2_), channel_id=1, source_target_pairs={{0,32},{8,40},{16,48},{24,56},{32,64},{40,72},{48,80},{56,88},{64,... | collective-permute-start | bytes 393224 | tf_op jit(solution)/shard_map/ppermute | solution.py:324
  26.6 7.0 %collective-permute-start.5 = (bf16[512,128]{1,0:T(8,128)(2,1)S(1)}, bf16[512,128]{1,0:T(8,128)(2,1)S(1)}, u32[]{:S(2)}, u32[]{:S(2)}) collective-permute-start(bf16[512,128]{1,0:T(8,128)(2,1)S(1)} %shard_map.66.refs_2_), channel_id=1, source_target_pairs={{0,96},{8,104},{16,112},{24,120},{32,0},{40,8},{48,16},{56,24},{64... | collective-permute-start | bytes 393224 | tf_op jit(solution)/shard_map/ppermute | solution.py:324
  28.8 7.0 %collective-permute-start.6 = (bf16[512,128]{1,0:T(8,128)(2,1)S(1)}, bf16[512,128]{1,0:T(8,128)(2,1)S(1)}, u32[]{:S(2)}, u32[]{:S(2)}) collective-permute-start(bf16[512,128]{1,0:T(8,128)(2,1)S(1)} %shard_map.66.refs_2_), channel_id=1, source_target_pairs={{0,64},{8,72},{16,80},{24,88},{32,96},{40,104},{48,112},{56,120},{... | collective-permute-start | bytes 393224 | tf_op jit(solution)/shard_map/ppermute | solution.py:324
  30.0 5.8 %copy-start = (f32[512]{0:T(512)S(1)}, f32[512]{0:T(512)}, u32[]{:S(2)}) copy-start(f32[512]{0:T(512)} %param.10) | copy-start | bytes 6148
  36.4 3.0 %collective-permute-start.7 = (bf16[512,512]{1,0:T(8,128)(2,1)S(1)}, bf16[512,512]{1,0:T(8,128)(2,1)S(1)}, u32[]{:S(2)}, u32[]{:S(2)}) collective-permute-start(bf16[512,512]{1,0:T(8,128)(2,1)S(1)} %shard_map.69), channel_id=1, source_target_pairs={{0,1},{1,0},{2,3},{3,2},{4,5},{5,4},{6,7},{7,6},{8,9},{9,8},{10,11... | collective-permute-start | bytes 1572872 | tf_op jit(solution)/shard_map/ppermute | solution.py:317
  40.7 13.7 %collective-permute-start.11 = (bf16[512,512]{1,0:T(8,128)(2,1)S(1)}, bf16[512,512]{1,0:T(8,128)(2,1)S(1)}, u32[]{:S(2)}, u32[]{:S(2)}) collective-permute-start(bf16[512,512]{1,0:T(8,128)(2,1)S(1)} %get-tuple-element.29), channel_id=1, source_target_pairs={{0,6},{1,7},{2,0},{3,1},{4,2},{5,3},{6,4},{7,5},{8,14},{9,15},{10,... | collective-permute-start | bytes 1572872 | tf_op jit(solution)/shard_map/ppermute | solution.py:317
  43.5 14.0 %collective-permute-start.12 = (bf16[512,512]{1,0:T(8,128)(2,1)S(1)}, bf16[512,512]{1,0:T(8,128)(2,1)S(1)}, u32[]{:S(2)}, u32[]{:S(2)}) collective-permute-start(bf16[512,512]{1,0:T(8,128)(2,1)S(1)} %get-tuple-element.30), channel_id=1, source_target_pairs={{0,2},{1,3},{2,4},{3,5},{4,6},{5,7},{6,0},{7,1},{8,10},{9,11},{10,... | collective-permute-start | bytes 1572872 | tf_op jit(solution)/shard_map/ppermute | solution.py:317
  44.7 22.0 %collective-permute-start.10 = (bf16[512,512]{1,0:T(8,128)(2,1)S(1)}, bf16[512,512]{1,0:T(8,128)(2,1)S(1)}, u32[]{:S(2)}, u32[]{:S(2)}) collective-permute-start(bf16[512,512]{1,0:T(8,128)(2,1)S(1)} %get-tuple-element.28), channel_id=1, source_target_pairs={{0,7},{1,6},{2,1},{3,0},{4,3},{5,2},{6,5},{7,4},{8,15},{9,14},{10,... | collective-permute-start | bytes 1572872 | tf_op jit(solution)/shard_map/ppermute | solution.py:317
  48.3 20.5 %collective-permute-start.9 = (bf16[512,512]{1,0:T(8,128)(2,1)S(1)}, bf16[512,512]{1,0:T(8,128)(2,1)S(1)}, u32[]{:S(2)}, u32[]{:S(2)}) collective-permute-start(bf16[512,512]{1,0:T(8,128)(2,1)S(1)} %get-tuple-element.27), channel_id=1, source_target_pairs={{0,2},{1,3},{2,4},{3,5},{4,6},{5,7},{6,0},{7,1},{8,10},{9,11},{10,... | collective-permute-start | bytes 1572872 | tf_op jit(solution)/shard_map/ppermute | solution.py:317
  49.5 19.2 %collective-permute-start.8 = (bf16[512,512]{1,0:T(8,128)(2,1)S(1)}, bf16[512,512]{1,0:T(8,128)(2,1)S(1)}, u32[]{:S(2)}, u32[]{:S(2)}) collective-permute-start(bf16[512,512]{1,0:T(8,128)(2,1)S(1)} %get-tuple-element.26), channel_id=1, source_target_pairs={{0,1},{1,0},{2,3},{3,2},{4,5},{5,4},{6,7},{7,6},{8,9},{9,8},{10,11... | collective-permute-start | bytes 1572872 | tf_op jit(solution)/shard_map/ppermute | solution.py:317
  58.8 18.1 %collective-permute-start.13 = (bf16[512,512]{1,0:T(8,128)(2,1)S(1)}, bf16[512,512]{1,0:T(8,128)(2,1)S(1)}, u32[]{:S(2)}, u32[]{:S(2)}) collective-permute-start(bf16[512,512]{1,0:T(8,128)(2,1)S(1)} %get-tuple-element.31), channel_id=1, source_target_pairs={{0,6},{1,7},{2,0},{3,1},{4,2},{5,3},{6,4},{7,5},{8,14},{9,15},{10,... | collective-permute-start | bytes 1572872 | tf_op jit(solution)/shard_map/ppermute | solution.py:317
  59.1 21.7 %collective-permute-start.14 = (bf16[512,512]{1,0:T(8,128)(2,1)S(1)}, bf16[512,512]{1,0:T(8,128)(2,1)S(1)}, u32[]{:S(2)}, u32[]{:S(2)}) collective-permute-start(bf16[512,512]{1,0:T(8,128)(2,1)S(1)} %get-tuple-element.32), channel_id=1, source_target_pairs={{0,3},{1,2},{2,5},{3,4},{4,7},{5,6},{6,1},{7,0},{8,11},{9,10},{10,... | collective-permute-start | bytes 1572872 | tf_op jit(solution)/shard_map/ppermute | solution.py:317
